TPU v7x, 512 devices: a whole 4x8x8 slice. The times are simulated.
512 devices in a mesh: beam: 32 (over y, x), trans: 16 (over z, core).
Axes of the slice: x: 4, y: 8, z: 8, core: 2. Of those that a mesh axis runs over, the one named last changes fastest.
Arguments:
- field_in: float32 [2, 128, 256, 256], P(None, 'beam', 'trans'), may hold values from -4 to 4
- phases: float32 [128, 4096], P('beam'), may hold values from -3.140625 to 3.140625
- energy: float32 [128, 4096], P('beam'), may hold values from -3 to 3
- row_cell: int32 [128, 4096], P('beam'), may hold values from 32 to 223
- col_cell: int32 [128, 4096], P('beam'), may hold values from 32 to 223
- weight: int32 [128, 4096], P('beam'), may hold values from 1 to 15
- charge: int32 [128], P('beam'), may hold values from 256 to 1024
- pole_rate: float32 [8], replicated, may hold values from 0.001953125 to 0.5
- pole_freq: float32 [8], replicated, may hold values from 0 to 0.3
- pole_amp: float32 [8], replicated, may hold values from -3 to 3
Outputs:
- field_out: float32 [2, 128, 256, 256], P(None, 'beam', 'trans')
- phase_out: float32 [128, 4096], P('beam')
- energy_out: float32 [128, 4096], P('beam')
All inputs are finite; a program needn't handle non-finite values.
Results may differ from a plain program's by a relative error of at most 0.00042.
Values sent between devices are 32-bit elements; how exact they have to be, the bound alone decides.
No kernel may reach another device: no remote copies, remote signals or barrier semaphores. Data moves between devices by JAX's collectives and lax.ppermute only.
A program may use at most 64 MiB of HBM per device.

v0:
```python
import functools
import math

import jax
import jax.numpy as jnp
from jax import lax
from jax.sharding import PartitionSpec as P

PERIODS = 2


diffraction = 20.0
kick_gain = 0.5
deposit_gain = 0.05
wake_gain = 3.0
charge_unit = 1024.0


def copy_for_each(shard, axis):
    length = lax.axis_size(axis)
    return lax.all_to_all(
        jnp.broadcast_to(shard[None], (length, *shard.shape)), axis, 0, 0, tiled=True
    )


def all_in_one(shard, axis):
    leaves = jax.tree.leaves(shard)
    order = sorted(range(len(leaves)), key=lambda k: -leaves[k].size)
    width = (1, *leaves[order[0]].shape)[-1]
    lines = [
        jnp.pad(leaves[k].reshape(-1), (0, -leaves[k].size % width)).reshape(-1, width)
        for k in order
    ]
    both, at, found = (copy_for_each(jnp.concatenate(lines), axis), 0, {})
    for k, line in zip(order, lines):
        section = both[:, at : at + len(line)].reshape(len(both), -1)
        found[k] = section[:, : leaves[k].size].reshape(-1, *leaves[k].shape)
        at += len(line)
    numbers = iter(range(len(leaves)))
    return jax.tree.map(lambda _: found[next(numbers)], shard)


def joined_by_halves(pieces, combine):
    while len(jax.tree.leaves(pieces)[0]) > 1:
        pieces = jax.vmap(combine)(
            *(jax.tree.map(lambda part: part[side::2], pieces) for side in (0, 1))
        )
    return jax.tree.map(lambda part: part[0], pieces)


def carried_in(shard, axis, combine, identity):
    length, mine = (lax.axis_size(axis), lax.axis_index(axis))
    passed = jnp.arange(length) < mine

    def kept(part, zero, own):
        part = jnp.where(
            passed.reshape(-1, *(1 for _ in own.shape)), part, jnp.asarray(zero, own.dtype)
        )
        return part

    pieces = all_in_one(shard, axis)
    return joined_by_halves(jax.tree.map(kept, pieces, identity, shard), combine)


def gathered_total(shard, axis):
    parts = lax.all_gather(shard, axis)
    return parts.sum(axis=0)


def shifted(value, axis, steps):
    count = lax.axis_size(axis)
    first, last = (max(0, -steps), min(count, count - steps))
    return lax.ppermute(value, axis, [(source, source + steps) for source in range(first, last)])


def complex_product(form, left_re, left_im, right_re, right_im):

    def single(first, second):
        return jnp.einsum(form, first, second, precision=lax.Precision.HIGHEST)

    return (
        single(left_re, right_re) - single(left_im, right_im),
        single(left_re, right_im) + single(left_im, right_re),
    )


def dft_table(length, sign):
    counter = jnp.arange(length, dtype=jnp.int32)
    product = counter[:, None] * counter[None, :] % length
    radians = 2.0 * math.pi / length * product.astype(jnp.float32)
    factor = 1.0 / math.sqrt(length)
    return (jnp.cos(radians) * factor, sign * jnp.sin(radians) * factor)


def propagator(row_index, col_index, length):

    def centred(index):
        return ((index + length // 2) % length - length // 2).astype(jnp.float32) / length

    radians = diffraction * (centred(row_index) ** 2 + centred(col_index) ** 2)
    return (jnp.cos(radians), -jnp.sin(radians))


def pole_power(steps, pole_rate, pole_freq):
    damping = jnp.exp(-pole_rate * steps)
    radians = pole_freq * steps
    return (damping * jnp.cos(radians), damping * jnp.sin(radians))


def wake_kicks(charge, pole_rate, pole_freq, pole_amp):
    members = charge.shape[0]
    groups = lax.axis_size("beam")
    charge_norm = charge.astype(jnp.float32) / charge_unit
    offsets = jnp.arange(members, dtype=jnp.float32)
    distance = offsets[:, None] - offsets[None, :]
    inner_re, inner_im = pole_power(jnp.maximum(distance, 0.0)[..., None], pole_rate, pole_freq)
    before = (distance > 0.0)[..., None]
    local_re = jnp.sum(jnp.where(before, inner_re, 0.0) * charge_norm[None, :, None], axis=1)
    tail_re, tail_im = pole_power((members - offsets)[:, None], pole_rate, pole_freq)
    block_re = jnp.sum(charge_norm[:, None] * tail_re, axis=0)
    block_im = jnp.sum(charge_norm[:, None] * tail_im, axis=0)
    whole_re, whole_im = pole_power(jnp.float32(members), pole_rate, pole_freq)

    def combine(first_part, second_part):
        first_are, first_aim, first_bre, first_bim = first_part
        second_are, second_aim, second_bre, second_bim = second_part
        return (
            first_are * second_are - first_aim * second_aim,
            first_are * second_aim + first_aim * second_are,
            second_are * first_bre - second_aim * first_bim + second_bre,
            second_are * first_bim + second_aim * first_bre + second_bim,
        )

    ones_like = jnp.ones_like(block_re)
    zeros_like = jnp.zeros_like(block_re)
    prefix = carried_in(
        (whole_re, whole_im, block_re, block_im),
        "beam",
        combine,
        (ones_like, zeros_like, zeros_like, zeros_like),
    )
    carry_re = prefix[2]
    carry_im = prefix[3]
    lead_re, lead_im = pole_power(offsets[:, None], pole_rate, pole_freq)
    state_re = local_re + lead_re * carry_re[None, :] - lead_im * carry_im[None, :]
    summed = jnp.sum(pole_amp[None, :] * (state_re + 0.5 * charge_norm[:, None]), axis=1)
    return wake_gain / (members * groups) * summed


def deposit_slice(band_rows, grid_cols, operands):
    local_row, column, part_re, part_im = operands
    row_hot = (local_row[:, None] == jnp.arange(band_rows, dtype=jnp.int32)[None, :]).astype(
        jnp.bfloat16
    )
    col_hot = (column[:, None] == jnp.arange(grid_cols, dtype=jnp.int32)[None, :]).astype(
        jnp.bfloat16
    )
    spread = jnp.concatenate([col_hot * part_re[:, None], col_hot * part_im[:, None]], axis=1)
    return lax.dot_general(
        row_hot, spread, (((0,), (0,)), ((), ())), preferred_element_type=jnp.float32
    )


def probe_slice(band_rows, grid_cols, operands):
    local_row, column, slab_re, slab_im = operands
    row_hot = (local_row[:, None] == jnp.arange(band_rows, dtype=jnp.int32)[None, :]).astype(
        jnp.float32
    )
    stacked = jnp.concatenate([slab_re, slab_im], axis=1)
    picked = jnp.dot(
        row_hot, stacked, precision=lax.Precision.HIGHEST, preferred_element_type=jnp.float32
    )
    col_hot = column[:, None] == jnp.arange(grid_cols, dtype=jnp.int32)[None, :]
    value_re = jnp.sum(jnp.where(col_hot, picked[:, :grid_cols], 0.0), axis=1)
    value_im = jnp.sum(jnp.where(col_hot, picked[:, grid_cols:], 0.0), axis=1)
    return (value_re, value_im)


def diffract(field_re, field_im, forward, inverse):
    cols_re, cols_im = complex_product("srn,nc->scr", field_re, field_im, forward[0], forward[1])
    halves = lax.all_to_all(
        jnp.stack([cols_re, cols_im]), "trans", split_axis=2, concat_axis=3, tiled=True
    )
    part_re = halves[0]
    part_im = halves[1]
    col_band = part_re.shape[1]
    grid_rows = part_re.shape[2]
    columns = lax.axis_index("trans") * col_band + jnp.arange(col_band, dtype=jnp.int32)
    spec_re, spec_im = complex_product("sqr,rk->sqk", part_re, part_im, forward[0], forward[1])
    kernel_re, kernel_im = propagator(
        jnp.arange(grid_rows, dtype=jnp.int32)[None, :], columns[:, None], grid_rows
    )
    moved_re = spec_re * kernel_re - spec_im * kernel_im
    moved_im = spec_re * kernel_im + spec_im * kernel_re
    back_re, back_im = complex_product("sqk,kr->sqr", moved_re, moved_im, inverse[0], inverse[1])
    rows_both = lax.all_to_all(
        jnp.stack([back_re, back_im]), "trans", split_axis=3, concat_axis=2, tiled=True
    )
    return complex_product("scr,cn->srn", rows_both[0], rows_both[1], inverse[0], inverse[1])


def shards(
    field_in, phases, energy, row_cell, col_cell, weight, charge, pole_rate, pole_freq, pole_amp
):
    field_re = field_in[0]
    field_im = field_in[1]
    slab_count, band_rows, grid_cols = field_re.shape
    row_start = lax.axis_index("trans") * band_rows
    wake_kick = wake_kicks(charge, pole_rate, pole_freq, pole_amp)
    charge_norm = charge.astype(jnp.float32) / charge_unit
    strength = (deposit_gain * charge_norm)[:, None, None]
    local_row = row_cell - row_start
    weights = weight.astype(jnp.float32)
    forward = dft_table(grid_cols, -1.0)
    inverse = dft_table(grid_cols, 1.0)
    depositor = functools.partial(deposit_slice, band_rows, grid_cols)
    reader = functools.partial(probe_slice, band_rows, grid_cols)
    angles = phases
    energies = energy
    for period in range(PERIODS):
        local_re, local_im = lax.map(reader, (local_row, col_cell, field_re, field_im))
        probed = gathered_total(jnp.stack([local_re, local_im]), "trans")
        energies = (
            energies
            - kick_gain * (probed[0] * jnp.cos(angles) - probed[1] * jnp.sin(angles))
            - wake_kick[:, None]
        )
        angles = angles + energies
        part_re = (weights * jnp.cos(angles)).astype(jnp.bfloat16)
        part_im = (-weights * jnp.sin(angles)).astype(jnp.bfloat16)
        bunched = lax.map(depositor, (local_row, col_cell, part_re, part_im))
        field_re = field_re + strength * bunched[:, :, :grid_cols]
        field_im = field_im + strength * bunched[:, :, grid_cols:]
        field_re, field_im = diffract(field_re, field_im, forward, inverse)
        head_slice = shifted(jnp.stack([field_re[-1], field_im[-1]]), "beam", 1)
        field_re = jnp.concatenate([head_slice[0][None], field_re[:-1]], axis=0)
        field_im = jnp.concatenate([head_slice[1][None], field_im[:-1]], axis=0)
    return (jnp.stack([field_re, field_im]), angles, energies)


def solution(mesh):
    placed = (
        P(None, "beam", "trans", None),
        P("beam", None),
        P("beam", None),
        P("beam", None),
        P("beam", None),
        P("beam", None),
        P("beam"),
        P(),
        P(),
        P(),
    )
    return jax.shard_map(
        shards,
        mesh=mesh,
        in_specs=placed,
        out_specs=(P(None, "beam", "trans", None), P("beam", None), P("beam", None)),
        check_vma=False,
    )
```

profile of v0, /device:TPU:32, one launch (start us, length us, event | category | flops | bytes accessed | tf_op | source)
XLA Modules:
  0.0 312.1 jit_solution(17203418531630962524)
XLA Ops:
  9.1 23.5 %while.44 = (s32[]{:T(128)}, f32[4,4096]{1,0:T(4,128)S(1)}, f32[4,4096]{1,0:T(4,128)S(1)}, s32[4,4096]{1,0:T(4,128)}, s32[4,4096]{1,0:T(4,128)S(1)}, /*index=5*/...) while((s32[]{:T(128)}, f32[4,4096]{1,0:T(4,128)S(1)}, f32[4,4096]{1,0:T(4,128)S(1)}, ...), condition=%wide.region_3.4_spmd, body=%wide.region_0.3_spmd.sunk | while | flops 407961600 | bytes 17072236 | solution.py:221
  10.0 3.5 %fusion.385 = f32[4096,512]{0,1:T(8,128)S(1)} fusion(s32[4096]{0:T(1024)S(1)} %bitcast.301, f32[16,256]{1,0:T(8,128)S(1)} %get-tuple-element.458, f32[16,256]{1,0:T(8,128)S(1)} %get-tuple-element.459), kind=kOutput, calls=%fused_computation.6.clone.1 | convolution fusion | flops 402726912 | bytes 8437760 | tf_op jit(solution)/shard_map/while/body/eval_jaxpr/dot_general | solution.py:170
  15.9 3.5 %fusion.385 = f32[4096,512]{0,1:T(8,128)S(1)} fusion(s32[4096]{0:T(1024)S(1)} %bitcast.301, f32[16,256]{1,0:T(8,128)S(1)} %get-tuple-element.458, f32[16,256]{1,0:T(8,128)S(1)} %get-tuple-element.459), kind=kOutput, calls=%fused_computation.6.clone.1 | convolution fusion | flops 402726912 | bytes 8437760 | tf_op jit(solution)/shard_map/while/body/eval_jaxpr/dot_general | solution.py:170
  21.7 3.5 %fusion.385 = f32[4096,512]{0,1:T(8,128)S(1)} fusion(s32[4096]{0:T(1024)S(1)} %bitcast.301, f32[16,256]{1,0:T(8,128)S(1)} %get-tuple-element.458, f32[16,256]{1,0:T(8,128)S(1)} %get-tuple-element.459), kind=kOutput, calls=%fused_computation.6.clone.1 | convolution fusion | flops 402726912 | bytes 8437760 | tf_op jit(solution)/shard_map/while/body/eval_jaxpr/dot_general | solution.py:170
  27.6 3.5 %fusion.385 = f32[4096,512]{0,1:T(8,128)S(1)} fusion(s32[4096]{0:T(1024)S(1)} %bitcast.301, f32[16,256]{1,0:T(8,128)S(1)} %get-tuple-element.458, f32[16,256]{1,0:T(8,128)S(1)} %get-tuple-element.459), kind=kOutput, calls=%fused_computation.6.clone.1 | convolution fusion | flops 402726912 | bytes 8437760 | tf_op jit(solution)/shard_map/while/body/eval_jaxpr/dot_general | solution.py:170
  34.1 10.2 %all-to-all-start = ((f32[32,4,8]{2,1,0:T(4,128)}), f32[32,4,8]{2,1,0:T(4,128)S(1)}, u32[]{:S(2)}, u32[]{:S(2)}) async-start(f32[32,4,8]{2,1,0:T(4,128)} %broadcast_in_dim.86), calls=%async_computation | async-start | bytes 131072 | tf_op jit(solution)/shard_map/all_to_all | solution.py:21
  44.5 4.9 %all-to-all-done = f32[32,4,8]{2,1,0:T(4,128)S(1)} async-done(((f32[32,4,8]{2,1,0:T(4,128)}), f32[32,4,8]{2,1,0:T(4,128)S(1)}, u32[]{:S(2)}, u32[]{:S(2)}) %all-to-all-start) | async-done | bytes 4128 | tf_op jit(solution)/shard_map/all_to_all | solution.py:21
  50.4 30.2 %all-gather.5.cloned.1.call-done = f32[32,4,4096]{2,1,0:T(4,128)} async-done(((f32[2,4,4096]{2,1,0:T(4,128)}), f32[32,4,4096]{2,1,0:T(4,128)}) %all-gather.5.cloned.1.call-update) | async-done | bytes 2097168 | tf_op jit(solution)/shard_map/all_gather | solution.py:66
  84.1 16.1 %while.45 = (s32[]{:T(128)}, f32[4,16,512]{2,1,0:T(8,128)S(1)}, s32[4,4096]{1,0:T(4,128)S(1)}, s32[4,4096]{1,0:T(4,128)S(1)}, bf16[4,4096]{1,0:T(4,128)(2,1)S(1)}, /*index=5*/bf16[4,4096]{1,0:T(4,128)(2,1)S(1)}, s32[]{:T(128)}) while((s32[]{:T(128)}, f32[4,16,512]{2,1,0:T(8,128)S(1)}, s32[4,4096]{1,0:T(4,128)S(1)}, ...), condition=%wide.region_10.11_spmd, body=%wide.region_9.10_spmd.sunk | while | flops 78708736 | bytes 8568921 | solution.py:231
  84.2 3.2 %fusion.388 = (bf16[4096,256]{1,0:T(8,128)(2,1)S(1)}, bf16[4096,256]{1,0:T(8,128)(2,1)S(1)}) fusion(s32[4096]{0:T(1024)S(1)} %bitcast.323, bf16[4096]{0:T(1024)(128)(2,1)S(1)} %get-tuple-element.470, bf16[4096]{0:T(1024)(128)(2,1)S(1)} %get-tuple-element.471), kind=kLoop, calls=%fused_computation.38.clone.1 | loop fusion | flops 3145728 | bytes 4227072 | tf_op jit(solution)/shard_map/while/body/eval_jaxpr/mul | solution.py:158
  88.3 3.2 %fusion.388 = (bf16[4096,256]{1,0:T(8,128)(2,1)S(1)}, bf16[4096,256]{1,0:T(8,128)(2,1)S(1)}) fusion(s32[4096]{0:T(1024)S(1)} %bitcast.323, bf16[4096]{0:T(1024)(128)(2,1)S(1)} %get-tuple-element.470, bf16[4096]{0:T(1024)(128)(2,1)S(1)} %get-tuple-element.471), kind=kLoop, calls=%fused_computation.38.clone.1 | loop fusion | flops 3145728 | bytes 4227072 | tf_op jit(solution)/shard_map/while/body/eval_jaxpr/mul | solution.py:158
  92.3 3.2 %fusion.388 = (bf16[4096,256]{1,0:T(8,128)(2,1)S(1)}, bf16[4096,256]{1,0:T(8,128)(2,1)S(1)}) fusion(s32[4096]{0:T(1024)S(1)} %bitcast.323, bf16[4096]{0:T(1024)(128)(2,1)S(1)} %get-tuple-element.470, bf16[4096]{0:T(1024)(128)(2,1)S(1)} %get-tuple-element.471), kind=kLoop, calls=%fused_computation.38.clone.1 | loop fusion | flops 3145728 | bytes 4227072 | tf_op jit(solution)/shard_map/while/body/eval_jaxpr/mul | solution.py:158
  96.3 3.2 %fusion.388 = (bf16[4096,256]{1,0:T(8,128)(2,1)S(1)}, bf16[4096,256]{1,0:T(8,128)(2,1)S(1)}) fusion(s32[4096]{0:T(1024)S(1)} %bitcast.323, bf16[4096]{0:T(1024)(128)(2,1)S(1)} %get-tuple-element.470, bf16[4096]{0:T(1024)(128)(2,1)S(1)} %get-tuple-element.471), kind=kLoop, calls=%fused_computation.38.clone.1 | loop fusion | flops 3145728 | bytes 4227072 | tf_op jit(solution)/shard_map/while/body/eval_jaxpr/mul | solution.py:158
  107.3 3.9 %all-to-all-start.1 = ((f32[16,1,2048]{2,1,0:T(1,128)}), f32[16,1,2048]{2,1,0:T(1,128)S(1)}, u32[]{:S(2)}, u32[]{:S(2)}) async-start(f32[16,1,2048]{2,1,0:T(1,128)} %reshape.254), calls=%async_computation.1 | async-start | bytes 262144 | tf_op jit(solution)/shard_map/all_to_all | solution.py:181
  111.7 8.2 %all-to-all-done.1 = f32[16,1,2048]{2,1,0:T(1,128)S(1)} async-done(((f32[16,1,2048]{2,1,0:T(1,128)}), f32[16,1,2048]{2,1,0:T(1,128)S(1)}, u32[]{:S(2)}, u32[]{:S(2)}) %all-to-all-start.1) | async-done | bytes 131104 | tf_op jit(solution)/shard_map/all_to_all | solution.py:181
  135.1 11.6 %all_to_all.65 = f32[16,1,2048]{2,1,0:T(1,128)S(1)} all-to-all(f32[16,1,2048]{2,1,0:T(1,128)S(1)} %reshape.256), channel_id=1, replica_groups=mesh['beam'=32,'trans'=16] {'trans'}, dimensions={0} | all-to-all | bytes 262144 | tf_op jit(solution)/shard_map/all_to_all | solution.py:196
  154.5 3.8 %collective-permute-start = (f32[2,16,256]{2,1,0:T(8,128)S(1)}, f32[2,16,256]{2,1,0:T(8,128)S(1)}, u32[]{:S(2)}, u32[]{:S(2)}) collective-permute-start(f32[2,16,256]{2,1,0:T(8,128)S(1)} %pad_maximum_fusion.9), channel_id=1, source_target_pairs={{0,16},{16,32},{32,48},{48,64},{64,80},{80,96},{96,112},{112,128},... | collective-permute-start | bytes 98312 | tf_op jit(solution)/shard_map/ppermute | solution.py:73
  158.4 5.3 %collective-permute-done = f32[2,16,256]{2,1,0:T(8,128)S(1)} collective-permute-done((f32[2,16,256]{2,1,0:T(8,128)S(1)}, f32[2,16,256]{2,1,0:T(8,128)S(1)}, u32[]{:S(2)}, u32[]{:S(2)}) %collective-permute-start) | collective-permute-done | bytes 32800 | tf_op jit(solution)/shard_map/ppermute | solution.py:73
  163.8 20.1 %while.46 = (s32[]{:T(128)}, f32[4,4096]{1,0:T(4,128)S(1)}, f32[4,4096]{1,0:T(4,128)S(1)}, s32[4,4096]{1,0:T(4,128)S(1)}, s32[4,4096]{1,0:T(4,128)S(1)}, /*index...) while((s32[]{:T(128)}, f32[4,4096]{1,0:T(4,128)S(1)}, ...), condition=%wide.region_14.15_spmd, body=%wide.region_11.14_spmd.sunk | while | flops 407961600 | bytes 17072236 | solution.py:221
  163.8 3.5 %fusion.391 = f32[4096,512]{0,1:T(8,128)S(1)} fusion(s32[4096]{0:T(1024)S(1)} %bitcast.302, f32[16,256]{1,0:T(8,128)S(1)} %get-tuple-element.483, f32[16,256]{1,0:T(8,128)S(1)} %get-tuple-element.484), kind=kOutput, calls=%fused_computation.22.clone.1 | convolution fusion | flops 402726912 | bytes 8437760 | tf_op jit(solution)/shard_map/while/body/eval_jaxpr/dot_general | solution.py:170
  168.8 3.5 %fusion.391 = f32[4096,512]{0,1:T(8,128)S(1)} fusion(s32[4096]{0:T(1024)S(1)} %bitcast.302, f32[16,256]{1,0:T(8,128)S(1)} %get-tuple-element.483, f32[16,256]{1,0:T(8,128)S(1)} %get-tuple-element.484), kind=kOutput, calls=%fused_computation.22.clone.1 | convolution fusion | flops 402726912 | bytes 8437760 | tf_op jit(solution)/shard_map/while/body/eval_jaxpr/dot_general | solution.py:170
  173.9 3.5 %fusion.391 = f32[4096,512]{0,1:T(8,128)S(1)} fusion(s32[4096]{0:T(1024)S(1)} %bitcast.302, f32[16,256]{1,0:T(8,128)S(1)} %get-tuple-element.483, f32[16,256]{1,0:T(8,128)S(1)} %get-tuple-element.484), kind=kOutput, calls=%fused_computation.22.clone.1 | convolution fusion | flops 402726912 | bytes 8437760 | tf_op jit(solution)/shard_map/while/body/eval_jaxpr/dot_general | solution.py:170
  178.9 3.5 %fusion.391 = f32[4096,512]{0,1:T(8,128)S(1)} fusion(s32[4096]{0:T(1024)S(1)} %bitcast.302, f32[16,256]{1,0:T(8,128)S(1)} %get-tuple-element.483, f32[16,256]{1,0:T(8,128)S(1)} %get-tuple-element.484), kind=kOutput, calls=%fused_computation.22.clone.1 | convolution fusion | flops 402726912 | bytes 8437760 | tf_op jit(solution)/shard_map/while/body/eval_jaxpr/dot_general | solution.py:170
  184.5 37.5 %all-gather.7.cloned.1.call-done = f32[32,4,4096]{2,1,0:T(4,128)} async-done(((f32[2,4,4096]{2,1,0:T(4,128)}), f32[32,4,4096]{2,1,0:T(4,128)}) %all-gather.7.cloned.1.call-update) | async-done | bytes 2097168 | tf_op jit(solution)/shard_map/all_gather | solution.py:66
  225.8 16.1 %while.47 = (s32[]{:T(128)}, f32[4,16,512]{2,1,0:T(8,128)S(1)}, s32[4,4096]{1,0:T(4,128)S(1)}, s32[4,4096]{1,0:T(4,128)S(1)}, bf16[4,4096]{1,0:T(4,128)(2,1)S(1)}, /*index=5*/bf16[4,4096]{1,0:T(4,128)(2,1)S(1)}, s32[]{:T(128)}) while((s32[]{:T(128)}, f32[4,16,512]{2,1,0:T(8,128)S(1)}, s32[4,4096]{1,0:T(4,128)S(1)}, ...), condition=%wide.region_17.18_spmd, body=%wide.region_16.17_spmd.sunk | while | flops 78708736 | bytes 8568921 | solution.py:231
  226.0 3.2 %fusion.394 = (bf16[4096,256]{1,0:T(8,128)(2,1)S(1)}, bf16[4096,256]{1,0:T(8,128)(2,1)S(1)}) fusion(s32[4096]{0:T(1024)S(1)} %bitcast.324, bf16[4096]{0:T(1024)(128)(2,1)S(1)} %get-tuple-element.495, bf16[4096]{0:T(1024)(128)(2,1)S(1)} %get-tuple-element.496), kind=kLoop, calls=%fused_computation.54.clone.1 | loop fusion | flops 3145728 | bytes 4227072 | tf_op jit(solution)/shard_map/while/body/eval_jaxpr/mul | solution.py:158
  230.0 3.2 %fusion.394 = (bf16[4096,256]{1,0:T(8,128)(2,1)S(1)}, bf16[4096,256]{1,0:T(8,128)(2,1)S(1)}) fusion(s32[4096]{0:T(1024)S(1)} %bitcast.324, bf16[4096]{0:T(1024)(128)(2,1)S(1)} %get-tuple-element.495, bf16[4096]{0:T(1024)(128)(2,1)S(1)} %get-tuple-element.496), kind=kLoop, calls=%fused_computation.54.clone.1 | loop fusion | flops 3145728 | bytes 4227072 | tf_op jit(solution)/shard_map/while/body/eval_jaxpr/mul | solution.py:158
  238.0 3.2 %fusion.394 = (bf16[4096,256]{1,0:T(8,128)(2,1)S(1)}, bf16[4096,256]{1,0:T(8,128)(2,1)S(1)}) fusion(s32[4096]{0:T(1024)S(1)} %bitcast.324, bf16[4096]{0:T(1024)(128)(2,1)S(1)} %get-tuple-element.495, bf16[4096]{0:T(1024)(128)(2,1)S(1)} %get-tuple-element.496), kind=kLoop, calls=%fused_computation.54.clone.1 | loop fusion | flops 3145728 | bytes 4227072 | tf_op jit(solution)/shard_map/while/body/eval_jaxpr/mul | solution.py:158
  248.4 12.7 %all_to_all.66 = f32[16,1,2048]{2,1,0:T(1,128)S(1)} all-to-all(f32[16,1,2048]{2,1,0:T(1,128)S(1)} %reshape.258), channel_id=1, replica_groups=mesh['beam'=32,'trans'=16] {'trans'}, dimensions={0} | all-to-all | bytes 262144 | tf_op jit(solution)/shard_map/all_to_all | solution.py:181
  275.5 11.6 %all_to_all.67 = f32[16,1,2048]{2,1,0:T(1,128)S(1)} all-to-all(f32[16,1,2048]{2,1,0:T(1,128)S(1)} %reshape.260), channel_id=1, replica_groups=mesh['beam'=32,'trans'=16] {'trans'}, dimensions={0} | all-to-all | bytes 262144 | tf_op jit(solution)/shard_map/all_to_all | solution.py:196
  295.0 3.4 %collective-permute-start.1 = (f32[2,16,256]{2,1,0:T(8,128)S(1)}, f32[2,16,256]{2,1,0:T(8,128)S(1)}, u32[]{:S(2)}, u32[]{:S(2)}) collective-permute-start(f32[2,16,256]{2,1,0:T(8,128)S(1)} %pad_maximum_fusion.10), channel_id=1, source_target_pairs={{0,16},{16,32},{32,48},{48,64},{64,80},{80,96},{96,112},{112,128},... | collective-permute-start | bytes 98312 | tf_op jit(solution)/shard_map/ppermute | solution.py:73
  298.4 5.7 %collective-permute-done.1 = f32[2,16,256]{2,1,0:T(8,128)S(1)} collective-permute-done((f32[2,16,256]{2,1,0:T(8,128)S(1)}, f32[2,16,256]{2,1,0:T(8,128)S(1)}, u32[]{:S(2)}, u32[]{:S(2)}) %collective-permute-start.1) | collective-permute-done | bytes 32800 | tf_op jit(solution)/shard_map/ppermute | solution.py:73
  (245 shorter events, 96.8 us)
Async XLA Ops:
  7.2 73.4 %all-gather.5.cloned.1.call-start = ((), (), s32[]{:S(2)}) async-start(), calls=%async_computation.5 | async-start | bytes 2228224 | tf_op jit(solution)/shard_map/all_gather | solution.py:66
  9.0 24.3 %copy-start.6 = (f32[8]{0:T(128)S(1)}, f32[8]{0:T(128)}, u32[]{:S(2)}) copy-start(f32[8]{0:T(128)} %param.26) | copy-start | bytes 100
  9.0 24.3 %copy-start.7 = (f32[8]{0:T(128)S(1)}, f32[8]{0:T(128)}, u32[]{:S(2)}) copy-start(f32[8]{0:T(128)} %param.25) | copy-start | bytes 100
  9.0 24.3 %copy-start.8 = (s32[4]{0:T(128)S(1)}, s32[4]{0:T(128)}, u32[]{:S(2)}) copy-start(s32[4]{0:T(128)} %param.24) | copy-start | bytes 52
  9.0 41.2 %copy-start.9 = (f32[8]{0:T(128)S(1)}, f32[8]{0:T(128)}, u32[]{:S(2)}) copy-start(f32[8]{0:T(128)} %param.27) | copy-start | bytes 100
  9.0 73.5 %copy-start.4 = (f32[4,4096]{1,0:T(4,128)S(1)}, f32[4,4096]{1,0:T(4,128)}, u32[]{:S(2)}) copy-start(f32[4,4096]{1,0:T(4,128)} %param.19) | copy-start | bytes 196612
  9.1 73.5 %copy-start.5 = (f32[4,4096]{1,0:T(4,128)S(1)}, f32[4,4096]{1,0:T(4,128)}, u32[]{:S(2)}) copy-start(f32[4,4096]{1,0:T(4,128)} %param.20) | copy-start | bytes 196612
  32.5 51.4 %copy-start.1 = (s32[4,4096]{1,0:T(4,128)S(1)}, s32[4,4096]{1,0:T(4,128)}, u32[]{:S(2)}) copy-start(s32[4,4096]{1,0:T(4,128)} %param.23) | copy-start | bytes 196612
  32.5 51.5 %copy-start = (s32[4,4096]{1,0:T(4,128)S(1)}, s32[4,4096]{1,0:T(4,128)}, u32[]{:S(2)}) copy-start(s32[4,4096]{1,0:T(4,128)} %get-tuple-element.603) | copy-start | bytes 196612
  34.1 15.3 %all-to-all-start = ((f32[32,4,8]{2,1,0:T(4,128)}), f32[32,4,8]{2,1,0:T(4,128)S(1)}, u32[]{:S(2)}, u32[]{:S(2)}) async-start(f32[32,4,8]{2,1,0:T(4,128)} %broadcast_in_dim.86), calls=%async_computation | async-start | bytes 131072 | tf_op jit(solution)/shard_map/all_to_all | solution.py:21
  84.1 16.1 %copy-start.3 = (f32[2,4,16,256]{3,2,1,0:T(8,128)S(1)}, f32[2,4,16,256]{3,2,1,0:T(8,128)}, u32[]{:S(2)}) copy-start(f32[2,4,16,256]{3,2,1,0:T(8,128)} %param.18) | copy-start | bytes 393220
  107.3 12.6 %all-to-all-start.1 = ((f32[16,1,2048]{2,1,0:T(1,128)}), f32[16,1,2048]{2,1,0:T(1,128)S(1)}, u32[]{:S(2)}, u32[]{:S(2)}) async-start(f32[16,1,2048]{2,1,0:T(1,128)} %reshape.254), calls=%async_computation.1 | async-start | bytes 262144 | tf_op jit(solution)/shard_map/all_to_all | solution.py:181
  111.2 110.9 %all-gather.7.cloned.1.call-start = ((), (), s32[]{:S(2)}) async-start(), calls=%async_computation.6 | async-start | bytes 2228224 | tf_op jit(solution)/shard_map/all_gather | solution.py:66
  154.5 9.2 %collective-permute-start = (f32[2,16,256]{2,1,0:T(8,128)S(1)}, f32[2,16,256]{2,1,0:T(8,128)S(1)}, u32[]{:S(2)}, u32[]{:S(2)}) collective-permute-start(f32[2,16,256]{2,1,0:T(8,128)S(1)} %pad_maximum_fusion.9), channel_id=1, source_target_pairs={{0,16},{16,32},{32,48},{48,64},{64,80},{80,96},{96,112},{112,128},... | collective-permute-start | bytes 98312 | tf_op jit(solution)/shard_map/ppermute | solution.py:73
  225.2 0.6 copy-start.2
  295.0 9.2 %collective-permute-start.1 = (f32[2,16,256]{2,1,0:T(8,128)S(1)}, f32[2,16,256]{2,1,0:T(8,128)S(1)}, u32[]{:S(2)}, u32[]{:S(2)}) collective-permute-start(f32[2,16,256]{2,1,0:T(8,128)S(1)} %pad_maximum_fusion.10), channel_id=1, source_target_pairs={{0,16},{16,32},{32,48},{48,64},{64,80},{80,96},{96,112},{112,128},... | collective-permute-start | bytes 98312 | tf_op jit(solution)/shard_map/ppermute | solution.py:73
Sparse Core Ops, SparseCore 0:
  33.4 47.1 all-gather.4
  184.7 37.3 all-gather.6
where the time goes:
time: 317 us; the launch traced here: 312 us
  waiting for transfers between devices  91.9 us (29%)
  matrix products  73.8 us (23%)
  other arithmetic  46.6 us (15%)
  blocking collectives  35.8 us (11%)
  local copies, waits for them, and re-layouts  26.7 us (8%)
  starting transfers between devices  21.6 us (7%)
  between operations  15.1 us (5%)
    all_gather x2, waiting for transfers between devices, gathered_total(): parts = lax.all_gather(shard, axis)  67.7 us
    dot_general x32, matrix products, single(): return jnp.einsum(form, first, second, precision=lax.Precision.HIGHEST)  40.4 us
    dot_general x8, matrix products, probe_slice(): jnp.dot(row_hot, stacked, precision=lax.Precision.HIGHEST, preferred_elem...  28.1 us
    mul x8, other arithmetic, deposit_slice(): col_hot * part_re[:, None]  25.6 us
    all_to_all x2, blocking collectives, diffract(): lax.all_to_all(jnp.stack([back_re, back_im]), 'trans', split_axis=3, conc...  23.1 us
    all_to_all x1, blocking collectives, diffract(): lax.all_to_all(jnp.stack([cols_re, cols_im]), 'trans', split_axis=2, conc...  12.7 us
    ppermute x2, waiting for transfers between devices, shifted(): lax.ppermute(value, axis, [(source, source + steps) for source in range(f...  11 us
    all_to_all x1, starting transfers between devices, copy_for_each(): lax.all_to_all(jnp.broadcast_to(shard[None], (length, *shard.shape)), axi...  10.2 us
  transfers between devices with their start and end apart: 6, of which 6 were waited for; matrix products, arithmetic and copies ran while one was open for 1% of the time, Pallas kernels for 0%

commit v1 on v0

v1 whole, which is shorter than its diff:
```python
import functools
import math

import jax
import jax.numpy as jnp
import numpy as np
from jax import lax
from jax.experimental import pallas as pl
from jax.experimental.pallas import tpu as pltpu
from jax.sharding import PartitionSpec as P

diffraction = 20.0
kick_gain = 0.5
deposit_gain = 0.05
wake_gain = 3.0
charge_unit = 1024.0

GRID = 256
SLICES = 128
NPART = 4096
BEAM = 32
TRANS = 16
LOW, HIGH = 32, 224
SPAN = HIGH - LOW
ROWS, WIDE = 8, 512
JOINT = ("beam", "trans")
QUADS = [[4 * r + c for c in range(4)] for r in range(4)]

f32 = jnp.float32
bf16 = jnp.bfloat16


def propagation_table():
    n = np.arange(GRID)
    centred = ((n + GRID // 2) % GRID - GRID // 2) / GRID
    k = np.exp(-1j * diffraction * centred**2)
    h = np.fft.ifft(k)
    a = h[(n[:, None] - n[None, :]) % GRID]
    parts = np.stack([a.real, a.imag]).astype(np.float32)
    high = parts.astype(jnp.bfloat16)
    low = (parts - high.astype(np.float32)).astype(jnp.bfloat16)
    return high, low


def moved(fn):
    out = []
    for b in range(BEAM):
        for t in range(TRANS):
            b2, t2 = fn(b, t)
            out.append((b * TRANS + t, (b2 % BEAM) * TRANS + t2))
    return out


FROM_EVEN = moved(lambda b, t: (b - 2 * t, t))
FROM_ODD = moved(lambda b, t: (b - 2 * t - 1, t))
TO_PREVIOUS = moved(lambda b, t: ((4 * b + t % 4 - 1) // 4, t // 4 * 4 + (t % 4 - 1) % 4))
NEXT_BEAM = [(b, (b + 1) % BEAM) for b in range(BEAM)]
NEXT_BEAM_PAIR = [
    (b * TRANS + t, (b + 1) % BEAM * TRANS + t)
    for b in range(BEAM)
    for t in range(TRANS)
    if t % 4 < 2
]


def split(x):
    high = x.astype(bf16)
    return high, (x - high.astype(f32)).astype(bf16)


def dot(a, b):
    return jnp.dot(a, b, preferred_element_type=f32)


def times_right(xr, xi, high, low):
    m = xr.shape[0]
    xh, xl = split(jnp.concatenate([xr, xi], axis=0))
    pr = dot(xh, high[0]) + dot(xl, high[0]) + dot(xh, low[0])
    pi = dot(xh, high[1]) + dot(xl, high[1]) + dot(xh, low[1])
    return pr[:m] - pi[m:], pi[:m] + pr[m:]


def times_left(ah, al, xr, xi):
    m = ah.shape[0] // 2
    rh, rl = split(xr)
    ih, il = split(xi)
    qr = dot(ah, rh) + dot(al, rh) + dot(ah, rl)
    qi = dot(ah, ih) + dot(al, ih) + dot(ah, il)
    return qr[:m] - qi[m:], qr[m:] + qi[:m]


def iota_rows(first, count):
    return lax.broadcasted_iota(jnp.int32, (count, WIDE), 0).astype(f32) + float(first)


def hot(values, rows_bf):
    return jnp.where(rows_bf == values.astype(bf16), jnp.ones((), bf16), jnp.zeros((), bf16))


def probe(fr, fi, rows, cols, out_re, out_im):
    high, low = split(jnp.concatenate([fr[LOW:HIGH], fi[LOW:HIGH]], axis=0))
    col_iota = iota_rows(0, GRID).astype(bf16)
    row_iota = iota_rows(LOW, SPAN)
    for q in range(ROWS):
        col_hot = hot(cols[q : q + 1], col_iota)
        found = dot(high, col_hot) + dot(low, col_hot)
        mask = row_iota == rows[q : q + 1]
        out_re[q : q + 1, :] = jnp.sum(jnp.where(mask, found[:SPAN], 0.0), axis=0, keepdims=True)
        out_im[q : q + 1, :] = jnp.sum(jnp.where(mask, found[SPAN:], 0.0), axis=0, keepdims=True)


def deposit(angles, weights, rows, cols):
    v = (weights * jnp.cos(angles)).astype(bf16)
    u = (-weights * jnp.sin(angles)).astype(bf16)
    col_iota = iota_rows(0, GRID).astype(bf16)
    row_iota = iota_rows(LOW, SPAN).astype(bf16)
    zero = jnp.zeros((), bf16)
    total = jnp.zeros((2 * SPAN, GRID), f32)
    for q in range(ROWS):
        col_hot = hot(cols[q : q + 1], col_iota)
        mask = row_iota == rows[q : q + 1].astype(bf16)
        left = jnp.concatenate(
            [jnp.where(mask, v[q : q + 1], zero), jnp.where(mask, u[q : q + 1], zero)], axis=0
        )
        total = total + lax.dot_general(
            left, col_hot, (((1,), (1,)), ((), ())), preferred_element_type=f32
        )
    return total[:SPAN], total[SPAN:]


def deposited(field, change, strength):
    return jnp.concatenate(
        [field[:LOW], field[LOW:HIGH] + strength * change, field[HIGH:]], axis=0
    )


def place():
    t = lax.axis_index("trans")
    return lax.axis_index("beam"), t, t % 4, t // 4


def prep_body(field, phases, energy, row, col, weight, charge, field_send, send, own, charges):
    _, _, c, _ = place()
    field_send[...] = field[:, 2:4]
    one, two = jnp.where(c == 0, 2, 3), 3
    own_one, own_two = jnp.maximum(c - 2, 0), jnp.maximum(c - 1, 0)

    def pick(ref, index, target, slot):
        line = ref[pl.ds(index, 1), :].astype(f32)
        for q in range(ROWS):
            target[slot, q : q + 1, :] = line[:, q * WIDE : (q + 1) * WIDE]

    for slot, ref in enumerate((phases, energy, row, col, weight)):
        pick(ref, one, send, slot)
        pick(ref, own_one, own, slot)
    for slot, ref in enumerate((row, col, weight)):
        pick(ref, two, send, 5 + slot)
        pick(ref, own_two, own, 5 + slot)
    lane = lax.broadcasted_iota(jnp.int32, (8, 128), 1) % 4
    line = jnp.zeros((8, 128), f32)
    for k in range(4):
        line = jnp.where(lane == k, charge[k].astype(f32) / charge_unit, line)
    charges[...] = line


def pack_body(field, shifted, even, odd, out):
    _, t, _, _ = place()
    lane = lax.broadcasted_iota(jnp.int32, (8, 128), 1) // 4
    top = lax.broadcasted_iota(jnp.int32, (8, 128), 0) == 0
    line = jnp.where(lane == 2 * t, even[...], jnp.where(lane == 2 * t + 1, odd[...], 0.0))
    line = jnp.where(top, line, 0.0)
    for c in range(4):
        for part in range(2):
            piece = shifted[part, c] if c < 2 else field[part, c - 2]
            for half in range(2):
                at = (part * 2 + half) * 16
                for r in range(4):
                    out[4 * r + c, at : at + 16, :] = piece[:, half * 128 : (half + 1) * 128]
    for t2 in range(TRANS):
        out[t2, 64:72, :] = line


def whole_field(x, part):
    halves = [
        x[:, (part * 2 + half) * 16 : (part * 2 + half + 1) * 16, :].reshape(GRID, 128)
        for half in range(2)
    ]
    return jnp.concatenate(halves, axis=1)


def chosen(own, received, slot, from_received):
    return jnp.where(from_received, received[slot], own[slot])


def first_body(x, own, received, rate, freq, amp, states, extra, re, im):
    b, _, c, _ = place()
    g = 4 * b + c
    take = lambda slot: chosen(own, received, slot, c < 2)
    fr, fi = whole_field(x, 0), whole_field(x, 1)
    probe(fr, fi, take(2), take(3), re, im)
    charges = jnp.sum(x[:, 64:72, :], axis=0)
    charges = jnp.sum(charges, axis=0, keepdims=True)
    source = (4 * b + lax.broadcasted_iota(jnp.int32, (8, 128), 1)) % SLICES
    pole = lax.broadcasted_iota(jnp.int32, (8, 128), 0)
    rates, freqs, amps = (jnp.zeros((8, 128), f32) for _ in range(3))
    for k in range(8):
        rates = jnp.where(pole == k, rate[k], rates)
        freqs = jnp.where(pole == k, freq[k], freqs)
        amps = jnp.where(pole == k, amp[k], amps)

    def total(value):
        return jnp.sum(jnp.sum(value, axis=0, keepdims=True), axis=1, keepdims=True)

    wakes, norms = [], []
    for back in (2, 1):
        s = (g + SLICES - back) % SLICES
        steps = jnp.maximum(s - source, 0).astype(f32)
        power = jnp.exp(-rates * steps) * jnp.cos(freqs * steps)
        reach = jnp.where(source < s, power, jnp.where(source == s, 0.5, 0.0))
        wakes.append(wake_gain / SLICES * total(amps * reach * charges))
        norms.append(total(jnp.where((source == s) & (pole == 0), charges, 0.0)))
    for k, value in enumerate((*wakes, *norms)):
        extra[k] = jnp.broadcast_to(value, (8, 128))
    angles = take(0)
    energies = (
        take(1) - kick_gain * (re[...] * jnp.cos(angles) - im[...] * jnp.sin(angles)) - wakes[0]
    )
    states[0] = angles + energies
    states[1] = energies


def second_body(x, states, own, received, extra, high, low, field, re, im):
    b, _, c, _ = place()
    take = lambda slot: chosen(own, received, slot, c < 2)
    br, bi = deposit(states[0], take(4), take(2), take(3))
    strength = deposit_gain * extra[2, 0:1, 0:1]
    fr = deposited(whole_field(x, 0), br, strength)
    fi = deposited(whole_field(x, 1), bi, strength)
    fr, fi = times_right(fr, fi, high, low)
    fr, fi = times_left(high[...].reshape(2 * GRID, GRID), low[...].reshape(2 * GRID, GRID), fr, fi)
    first = (b == 0) & (c == 1)
    fr = jnp.where(first, 0.0, fr)
    fi = jnp.where(first, 0.0, fi)
    field[0] = fr
    field[1] = fi
    take = lambda slot: chosen(own, received, slot, c < 1)
    probe(fr, fi, take(5), take(6), re, im)


def third_body(states, extra, re, im, out):
    angles = states[0]
    energies = (
        states[1]
        - kick_gain * (re[...] * jnp.cos(angles) - im[...] * jnp.sin(angles))
        - extra[1, 0:1, 0:1]
    )
    out[0] = angles + energies
    out[1] = energies


def fourth_body(field, states, own, received, extra, high, low, out):
    b, _, c, r = place()
    take = lambda slot: chosen(own, received, slot, c < 1)
    br, bi = deposit(states[0], take(7), take(5), take(6))
    strength = deposit_gain * extra[3, 0:1, 0:1]
    fr = deposited(field[0], br, strength)
    fi = deposited(field[1], bi, strength)
    at = pl.multiple_of(r * 64, 64)
    ah = jnp.concatenate([high[0, pl.ds(at, 64), :], high[1, pl.ds(at, 64), :]], axis=0)
    al = jnp.concatenate([low[0, pl.ds(at, 64), :], low[1, pl.ds(at, 64), :]], axis=0)
    fr, fi = times_left(ah, al, fr, fi)
    fr, fi = times_right(fr, fi, high, low)
    empty = (b == 0) & (c == 0)
    for part, value in enumerate((fr, fi)):
        value = jnp.where(empty, 0.0, value)
        for j in range(4):
            out[j, part * 16 : part * 16 + 16, :] = value[16 * j : 16 * j + 16]


def last_body(x, field, phase, energy):
    for c in range(4):
        for part in range(2):
            field[part, c] = x[c, part * 16 : part * 16 + 16, :]
        for k, target in enumerate((phase, energy)):
            for half in range(2):
                at = 32 + (k * 2 + half) * 8
                piece = x[c, at : at + 8, :]
                for q in range(ROWS):
                    begin = q * WIDE + half * 256
                    target[c : c + 1, begin : begin + 256] = piece[q : q + 1]


def call(body, outs, *args, scalars=(), scratch=()):
    specs = [
        pl.BlockSpec(memory_space=pltpu.SMEM if k in scalars else pltpu.VMEM)
        for k in range(len(args))
    ]
    return pl.pallas_call(
        body,
        out_shape=[jax.ShapeDtypeStruct(shape, f32) for shape in outs],
        in_specs=specs,
        out_specs=[pl.BlockSpec(memory_space=pltpu.VMEM) for _ in outs],
        scratch_shapes=list(scratch),
    )(*args)


def shards(
    field_in, phases, energy, row_cell, col_cell, weight, charge, pole_rate, pole_freq, pole_amp
):
    high, low = propagation_table()
    high, low = jnp.asarray(high), jnp.asarray(low)
    kept = (8, ROWS, WIDE)
    state_shape = (2, ROWS, WIDE)
    line = (ROWS, WIDE)
    field_send, send, own, charges = call(
        prep_body,
        [(2, 2, 16, GRID), kept, kept, (8, 128)],
        field_in, phases, energy, row_cell, col_cell, weight, charge,
        scalars=(6,),
    )
    shifted = lax.ppermute(field_send, "beam", NEXT_BEAM)
    even = lax.ppermute(charges, JOINT, FROM_EVEN)
    odd = lax.ppermute(charges, JOINT, FROM_ODD)
    received = lax.ppermute(send, JOINT, NEXT_BEAM_PAIR)
    (packed,) = call(pack_body, [(TRANS, 72, 128)], field_in, shifted, even, odd)
    x = lax.all_to_all(packed, "trans", 0, 0, tiled=True)
    states, extra, _, _ = call(
        first_body,
        [state_shape, (4, 8, 128), line, line],
        x, own, received, pole_rate, pole_freq, pole_amp,
        scalars=(3, 4, 5),
    )
    following = lax.ppermute(states, JOINT, TO_PREVIOUS)
    field, re, im = call(
        second_body,
        [(2, GRID, GRID), line, line],
        x, states, own, received, extra, high, low,
    )
    (final,) = call(third_body, [state_shape], following, extra, re, im)
    home = lax.ppermute(final, JOINT, TO_PREVIOUS)
    (bands,) = call(
        fourth_body, [(4, 32, GRID)], field, final, own, received, extra, high, low
    )
    home = jnp.concatenate([home[..., :256], home[..., 256:]], axis=1).reshape(32, 256)
    both = jnp.concatenate([bands, jnp.broadcast_to(home[None], (4, 32, 256))], axis=1)
    y = lax.all_to_all(both, "trans", 0, 0, tiled=True, axis_index_groups=QUADS)
    return tuple(
        call(last_body, [(2, 4, 16, GRID), (4, NPART), (4, NPART)], y)
    )


def solution(mesh):
    placed = (
        P(None, "beam", "trans", None),
        P("beam", None),
        P("beam", None),
        P("beam", None),
        P("beam", None),
        P("beam", None),
        P("beam"),
        P(),
        P(),
        P(),
    )
    return jax.shard_map(
        shards,
        mesh=mesh,
        in_specs=placed,
        out_specs=(P(None, "beam", "trans", None), P("beam", None), P("beam", None)),
        check_vma=False,
    )
```

time: 317 us -> 91.5 us (0.29)
  the two profiles are of different devices: /device:TPU:32 before, /device:TPU:1 now
where the time goes in v1:
time: 91.5 us; the launch traced here: 90.9 us
  starting transfers between devices  37.7 us (41%)
  Pallas kernels  21.9 us (24%)
  waiting for transfers between devices  18.5 us (20%)
  blocking collectives  8.52 us (9%)
  local copies, waits for them, and re-layouts  3.54 us (4%)
    pallas_call x7, Pallas kernels, call(): pl.pallas_call(body, out_shape=[jax.ShapeDtypeStruct(shape, f32) for shap...  21.9 us
    all_to_all x1, starting transfers between devices, shards(): x = lax.all_to_all(packed, 'trans', 0, 0, tiled=True)  17.7 us
    all_to_all x1, blocking collectives, shards(): y = lax.all_to_all(both, 'trans', 0, 0, tiled=True, axis_index_groups=QUADS)  8.52 us
    all_to_all x1, waiting for transfers between devices, shards(): x = lax.all_to_all(packed, 'trans', 0, 0, tiled=True)  8.36 us
    ppermute x1, waiting for transfers between devices, shards(): received = lax.ppermute(send, JOINT, NEXT_BEAM_PAIR)  8.24 us
    ppermute x1, starting transfers between devices, shards(): odd = lax.ppermute(charges, JOINT, FROM_ODD)  6.02 us
    ppermute x1, starting transfers between devices, shards(): even = lax.ppermute(charges, JOINT, FROM_EVEN)  4.24 us
    ppermute x1, starting transfers between devices, shards(): shifted = lax.ppermute(field_send, 'beam', NEXT_BEAM)  3.93 us
  transfers between devices with their start and end apart: 7, of which 3 were waited for; matrix products, arithmetic and copies ran while one was open for 0% of the time, Pallas kernels for 12%

profile of v1, /device:TPU:1, one launch (start us, length us, event | category | flops | bytes accessed | tf_op | source)
XLA Modules:
  0.0 90.9 jit_solution(12063389834954198146)
XLA Ops:
  0.6 1.8 %shard_map.139 = (f32[2,2,16,256]{3,2,1,0:T(8,128)}, f32[8,8,512]{2,1,0:T(8,128)}, f32[8,8,512]{2,1,0:T(8,128)}, f32[8,128]{1,0:T(8,128)}) custom-call(f32[2,4,16,256]{3,2,1,0:T(8,128)} %field.3, f32[4,4096]{1,0:T(4,128)} %phases.1, f32[4,4096]{1,0:T(4,128)} %energy.1, s32[4,4096]{1,0:T(4,128)} %row.1, s32[4,4096]{1,0:T(4,128)} %col.1, s32[4,4096]{1,0:T(4,128)} %weight.1, ...), custom_call_target="tpu_custom_call" | custom-call | tf_op jit(solution)/shard_map/pallas_call | solution.py:298
  2.5 3.9 %collective-permute-start = (f32[2,2,16,256]{3,2,1,0:T(8,128)}, f32[2,2,16,256]{3,2,1,0:T(8,128)S(1)}, u32[]{:S(2)}, u32[]{:S(2)}) collective-permute-start(f32[2,2,16,256]{3,2,1,0:T(8,128)} %get-tuple-element.12), channel_id=1, source_target_pairs={{0,16},{16,32},{32,48},{48,64},{64,80},{80,96},{96,112},{112,128},... | collective-permute-start | bytes 196616 | tf_op jit(solution)/shard_map/ppermute | solution.py:321
  6.4 6.0 %collective-permute-start.2 = (f32[8,128]{1,0:T(8,128)}, f32[8,128]{1,0:T(8,128)S(1)}, u32[]{:S(2)}, u32[]{:S(2)}) collective-permute-start(f32[8,128]{1,0:T(8,128)} %get-tuple-element.13), channel_id=1, source_target_pairs={{0,496},{1,465},{2,434},{3,403},{4,372},{5,341},{6,310},{7,279},{8... | collective-permute-start | bytes 12296 | tf_op jit(solution)/shard_map/ppermute | solution.py:323
  12.4 4.2 %collective-permute-start.1 = (f32[8,128]{1,0:T(8,128)}, f32[8,128]{1,0:T(8,128)S(1)}, u32[]{:S(2)}, u32[]{:S(2)}) collective-permute-start(f32[8,128]{1,0:T(8,128)} %get-tuple-element.13), channel_id=1, source_target_pairs={{0,0},{1,481},{2,450},{3,419},{4,388},{5,357},{6,326},{7,295},{8,2... | collective-permute-start | bytes 12296 | tf_op jit(solution)/shard_map/ppermute | solution.py:322
  16.7 0.0 collective-permute-done.2.odd
  16.7 0.0 copy-start.5
  16.7 1.9 %collective-permute-done.1.even = f32[8,128]{1,0:T(8,128)S(1)} collective-permute-done((f32[8,128]{1,0:T(8,128)}, f32[8,128]{1,0:T(8,128)S(1)}, u32[]{:S(2)}, u32[]{:S(2)}) %collective-permute-start.1) | collective-permute-done | bytes 4128 | tf_op jit(solution)/shard_map/ppermute | solution.py:322
  18.6 0.0 collective-permute-done.shifted
  18.6 0.0 copy-done.5
  18.6 0.6 copy-done.6
  19.2 0.6 copy-done.3
  19.8 1.8 %shard_map.140 = f32[16,72,128]{2,1,0:T(8,128)} custom-call(f32[2,4,16,256]{3,2,1,0:T(8,128)} %field.3, f32[2,2,16,256]{3,2,1,0:T(8,128)} %copy-done.3, f32[8,128]{1,0:T(8,128)} %copy-done.6, f32[8,128]{1,0:T(8,128)} %copy-done.5), custom_call_target="tpu_custom_call" | custom-call | tf_op jit(solution)/shard_map/pallas_call | solution.py:298
  21.6 17.7 %all-to-all-start = ((f32[16,72,128]{2,1,0:T(8,128)}), f32[16,72,128]{2,1,0:T(8,128)S(1)}, u32[]{:S(2)}, u32[]{:S(2)}) async-start(f32[16,72,128]{2,1,0:T(8,128)} %shard_map.140), calls=%async_computation | async-start | bytes 1179648 | tf_op jit(solution)/shard_map/all_to_all | solution.py:326
  39.3 0.0 copy-done.7
  39.4 1.9 %collective-permute-start.3 = (f32[8,8,512]{2,1,0:T(8,128)S(1)}, f32[8,8,512]{2,1,0:T(8,128)S(1)}, u32[]{:S(2)}, u32[]{:S(2)}) collective-permute-start(f32[8,8,512]{2,1,0:T(8,128)S(1)} %copy-done.7), channel_id=1, source_target_pairs={{0,16},{1,17},{4,20},{5,21},{8,24},{9,25},{12,28},{13,29},{16,32},... | collective-permute-start | bytes 393224 | tf_op jit(solution)/shard_map/ppermute | solution.py:324
  41.3 8.2 %collective-permute-done.3.received = f32[8,8,512]{2,1,0:T(8,128)S(1)} collective-permute-done((f32[8,8,512]{2,1,0:T(8,128)S(1)}, f32[8,8,512]{2,1,0:T(8,128)S(1)}, u32[]{:S(2)}, u32[]{:S(2)}) %collective-permute-start.3) | collective-permute-done | bytes 131104 | tf_op jit(solution)/shard_map/ppermute | solution.py:324
  49.5 8.4 %all-to-all-done.x = f32[16,72,128]{2,1,0:T(8,128)S(1)} async-done(((f32[16,72,128]{2,1,0:T(8,128)}), f32[16,72,128]{2,1,0:T(8,128)S(1)}, u32[]{:S(2)}, u32[]{:S(2)}) %all-to-all-start) | async-done | bytes 589856 | tf_op jit(solution)/shard_map/all_to_all | solution.py:326
  57.9 0.0 copy-done.1
  57.9 0.8 copy-done
  58.7 3.9 %shard_map.141 = (f32[2,8,512]{2,1,0:T(8,128)}, f32[4,8,128]{2,1,0:T(8,128)}, f32[8,512]{1,0:T(8,128)}, f32[8,512]{1,0:T(8,128)}) custom-call(f32[16,72,128]{2,1,0:T(8,128)} %copy-done, f32[8,8,512]{2,1,0:T(8,128)} %get-tuple-element.14.own, f32[8,8,512]{2,1,0:T(8,128)} %copy-done.1, f32[8]{0:T(128)} %rate.1, f32[8]{0:T(128)} %freq.1, f32[8]{0:T(128)} %amp.1), custom_call_target="tpu_custom_call" | custom-call | tf_op jit(solution)/shard_map/pallas_call | solution.py:298
  62.6 1.9 %collective-permute-start.4 = (f32[2,8,512]{2,1,0:T(8,128)}, f32[2,8,512]{2,1,0:T(8,128)S(1)}, u32[]{:S(2)}, u32[]{:S(2)}) collective-permute-start(f32[2,8,512]{2,1,0:T(8,128)} %get-tuple-element.16.states), channel_id=1, source_target_pairs={{0,499},{1,0},{2,1},{3,2},{4,503},{5,4},{6,5},{7,6},{8,507},{9,8},... | collective-permute-start | bytes 98312 | tf_op jit(solution)/shard_map/ppermute | solution.py:333
  64.5 7.4 %shard_map.142 = (f32[2,256,256]{2,1,0:T(8,128)}, f32[8,512]{1,0:T(8,128)}, f32[8,512]{1,0:T(8,128)}) custom-call(f32[16,72,128]{2,1,0:T(8,128)} %copy-done, f32[2,8,512]{2,1,0:T(8,128)} %get-tuple-element.16.states, f32[8,8,512]{2,1,0:T(8,128)} %get-tuple-element.14.own, f32[8,8,512]{2,1,0:T(8,128)} %copy-done.1, f32[4,8,128]{2,1,0:T(8,128)} %get-tuple-element.17.extra, ...), custom_call_target="tpu_custom_call" | custom-call | tf_op jit(solution)/shard_map/pallas_call | solution.py:298
  71.9 0.0 collective-permute-done.4.states
  71.9 0.6 copy-done.4
  72.5 1.5 %shard_map.143.states = f32[2,8,512]{2,1,0:T(8,128)} custom-call(f32[2,8,512]{2,1,0:T(8,128)} %copy-done.4, f32[4,8,128]{2,1,0:T(8,128)} %get-tuple-element.17.extra, f32[8,512]{1,0:T(8,128)} %get-tuple-element.19.re, f32[8,512]{1,0:T(8,128)} %get-tuple-element.20.im), custom_call_target="tpu_custom_call" | custom-call | tf_op jit(solution)/shard_map/pallas_call | solution.py:298
  74.0 1.9 %collective-permute-start.5 = (f32[2,8,512]{2,1,0:T(8,128)}, f32[2,8,512]{2,1,0:T(8,128)S(1)}, u32[]{:S(2)}, u32[]{:S(2)}) collective-permute-start(f32[2,8,512]{2,1,0:T(8,128)} %shard_map.143.states), channel_id=1, source_target_pairs={{0,499},{1,0},{2,1},{3,2},{4,503},{5,4},{6,5},{7,6},{8,507},{9,8},... | collective-permute-start | bytes 98312 | tf_op jit(solution)/shard_map/ppermute | solution.py:340
  75.9 3.8 %shard_map.144 = f32[4,32,256]{2,1,0:T(8,128)} custom-call(f32[2,256,256]{2,1,0:T(8,128)} %get-tuple-element.18.field, f32[2,8,512]{2,1,0:T(8,128)} %shard_map.143.states, f32[8,8,512]{2,1,0:T(8,128)} %get-tuple-element.14.own, f32[8,8,512]{2,1,0:T(8,128)} %copy-done.1, f32[4,8,128]{2,1,0:T(8,128)} %get-tuple-element.17.extra, ...), custom_call_target="tpu_custom_call" | custom-call | tf_op jit(solution)/shard_map/pallas_call | solution.py:298
  79.8 0.0 collective-permute-done.5
  79.8 0.0 copy-start.2
  79.8 0.9 copy-done.2
  80.7 8.5 %all_to_all.10.x = f32[4,64,256]{2,1,0:T(8,128)} all-to-all(f32[4,64,256]{2,1,0:T(8,128)S(1)} %pad_maximum_fusion), channel_id=1, replica_groups={{0,1,2,3},{4,5,6,7},{8,9,10,11},{12,13,14,15},{16,17,18,19},{20,21,22,2..., dimensions={0} | all-to-all | bytes 524288 | tf_op jit(solution)/shard_map/all_to_all | solution.py:346
  89.2 1.7 %shard_map.145 = (f32[2,4,16,256]{3,2,1,0:T(8,128)}, f32[4,4096]{1,0:T(4,128)}, f32[4,4096]{1,0:T(4,128)}) custom-call(f32[4,64,256]{2,1,0:T(8,128)} %all_to_all.10.x), custom_call_target="tpu_custom_call" | custom-call | tf_op jit(solution)/shard_map/pallas_call | solution.py:298
  (10 shorter events, 0.0 us)
Async XLA Ops:
  2.5 16.1 %collective-permute-start = (f32[2,2,16,256]{3,2,1,0:T(8,128)}, f32[2,2,16,256]{3,2,1,0:T(8,128)S(1)}, u32[]{:S(2)}, u32[]{:S(2)}) collective-permute-start(f32[2,2,16,256]{3,2,1,0:T(8,128)} %get-tuple-element.12), channel_id=1, source_target_pairs={{0,16},{16,32},{32,48},{48,64},{64,80},{80,96},{96,112},{112,128},... | collective-permute-start | bytes 196616 | tf_op jit(solution)/shard_map/ppermute | solution.py:321
  6.4 10.3 %collective-permute-start.2 = (f32[8,128]{1,0:T(8,128)}, f32[8,128]{1,0:T(8,128)S(1)}, u32[]{:S(2)}, u32[]{:S(2)}) collective-permute-start(f32[8,128]{1,0:T(8,128)} %get-tuple-element.13), channel_id=1, source_target_pairs={{0,496},{1,465},{2,434},{3,403},{4,372},{5,341},{6,310},{7,279},{8... | collective-permute-start | bytes 12296 | tf_op jit(solution)/shard_map/ppermute | solution.py:323
  12.4 6.2 %collective-permute-start.1 = (f32[8,128]{1,0:T(8,128)}, f32[8,128]{1,0:T(8,128)S(1)}, u32[]{:S(2)}, u32[]{:S(2)}) collective-permute-start(f32[8,128]{1,0:T(8,128)} %get-tuple-element.13), channel_id=1, source_target_pairs={{0,0},{1,481},{2,450},{3,419},{4,388},{5,357},{6,326},{7,295},{8,2... | collective-permute-start | bytes 12296 | tf_op jit(solution)/shard_map/ppermute | solution.py:322
  16.7 1.9 %copy-start.5 = (f32[8,128]{1,0:T(8,128)}, f32[8,128]{1,0:T(8,128)S(1)}, u32[]{:S(2)}) copy-start(f32[8,128]{1,0:T(8,128)S(1)} %collective-permute-done.2.odd) | copy-start | bytes 12292
  18.6 0.6 copy-start.6
  19.2 0.6 copy-start.3
  21.6 17.7 %copy-start.7 = (f32[8,8,512]{2,1,0:T(8,128)S(1)}, f32[8,8,512]{2,1,0:T(8,128)}, u32[]{:S(2)}) copy-start(f32[8,8,512]{2,1,0:T(8,128)} %get-tuple-element.15) | copy-start | bytes 393220
  21.6 36.3 %all-to-all-start = ((f32[16,72,128]{2,1,0:T(8,128)}), f32[16,72,128]{2,1,0:T(8,128)S(1)}, u32[]{:S(2)}, u32[]{:S(2)}) async-start(f32[16,72,128]{2,1,0:T(8,128)} %shard_map.140), calls=%async_computation | async-start | bytes 1179648 | tf_op jit(solution)/shard_map/all_to_all | solution.py:326
  39.4 10.2 %collective-permute-start.3 = (f32[8,8,512]{2,1,0:T(8,128)S(1)}, f32[8,8,512]{2,1,0:T(8,128)S(1)}, u32[]{:S(2)}, u32[]{:S(2)}) collective-permute-start(f32[8,8,512]{2,1,0:T(8,128)S(1)} %copy-done.7), channel_id=1, source_target_pairs={{0,16},{1,17},{4,20},{5,21},{8,24},{9,25},{12,28},{13,29},{16,32},... | collective-permute-start | bytes 393224 | tf_op jit(solution)/shard_map/ppermute | solution.py:324
  49.5 8.4 %copy-start.1 = (f32[8,8,512]{2,1,0:T(8,128)}, f32[8,8,512]{2,1,0:T(8,128)S(1)}, u32[]{:S(2)}) copy-start(f32[8,8,512]{2,1,0:T(8,128)S(1)} %collective-permute-done.3.received) | copy-start | bytes 393220
  57.9 0.8 copy-start
  62.6 9.4 %collective-permute-start.4 = (f32[2,8,512]{2,1,0:T(8,128)}, f32[2,8,512]{2,1,0:T(8,128)S(1)}, u32[]{:S(2)}, u32[]{:S(2)}) collective-permute-start(f32[2,8,512]{2,1,0:T(8,128)} %get-tuple-element.16.states), channel_id=1, source_target_pairs={{0,499},{1,0},{2,1},{3,2},{4,503},{5,4},{6,5},{7,6},{8,507},{9,8},... | collective-permute-start | bytes 98312 | tf_op jit(solution)/shard_map/ppermute | solution.py:333
  71.9 0.6 copy-start.4
  74.0 5.7 %collective-permute-start.5 = (f32[2,8,512]{2,1,0:T(8,128)}, f32[2,8,512]{2,1,0:T(8,128)S(1)}, u32[]{:S(2)}, u32[]{:S(2)}) collective-permute-start(f32[2,8,512]{2,1,0:T(8,128)} %shard_map.143.states), channel_id=1, source_target_pairs={{0,499},{1,0},{2,1},{3,2},{4,503},{5,4},{6,5},{7,6},{8,507},{9,8},... | collective-permute-start | bytes 98312 | tf_op jit(solution)/shard_map/ppermute | solution.py:340
  79.8 0.9 copy-start.2

commit v2 on v1

--- a/solution.py
+++ b/solution.py
@@ -51,11 +51,18 @@
     return out
 
 
-FROM_EVEN = moved(lambda b, t: (b - 2 * t, t))
-FROM_ODD = moved(lambda b, t: (b - 2 * t - 1, t))
+SPREAD = (
+    (1, 4, 5), (3, 8, 11), (12, 20, 24), (7, 27, 28), (9, 16, 25), (2, 21, 23),
+    (14, 19, 29), (15, 17, 30), (13, 18, 31), (6, 26, 28), (10, 22, 28),
+)
+FOURS = [
+    [m * TRANS + t for m in group]
+    for t in range(TRANS)
+    for group in sorted({tuple(sorted([b, *(b ^ v for v in SPREAD[t % 11])])) for b in range(BEAM)})
+]
 TO_PREVIOUS = moved(lambda b, t: ((4 * b + t % 4 - 1) // 4, t // 4 * 4 + (t % 4 - 1) % 4))
 NEXT_BEAM = [(b, (b + 1) % BEAM) for b in range(BEAM)]
-NEXT_BEAM_PAIR = [
+PAIR_TO_NEXT = [
     (b * TRANS + t, (b + 1) % BEAM * TRANS + t)
     for b in range(BEAM)
     for t in range(TRANS)
@@ -139,9 +146,8 @@
     return lax.axis_index("beam"), t, t % 4, t // 4
 
 
-def prep_body(field, phases, energy, row, col, weight, charge, field_send, send, own, charges):
-    _, _, c, _ = place()
-    field_send[...] = field[:, 2:4]
+def prep_body(phases, energy, row, col, weight, charge, send, own, charges):
+    b, _, c, _ = place()
     one, two = jnp.where(c == 0, 2, 3), 3
     own_one, own_two = jnp.maximum(c - 2, 0), jnp.maximum(c - 1, 0)
 
@@ -156,28 +162,25 @@
     for slot, ref in enumerate((row, col, weight)):
         pick(ref, two, send, 5 + slot)
         pick(ref, own_two, own, 5 + slot)
-    lane = lax.broadcasted_iota(jnp.int32, (8, 128), 1) % 4
+    lane = lax.broadcasted_iota(jnp.int32, (8, 128), 1)
     line = jnp.zeros((8, 128), f32)
     for k in range(4):
-        line = jnp.where(lane == k, charge[k].astype(f32) / charge_unit, line)
-    charges[...] = line
-
-
-def pack_body(field, shifted, even, odd, out):
-    _, t, _, _ = place()
-    lane = lax.broadcasted_iota(jnp.int32, (8, 128), 1) // 4
-    top = lax.broadcasted_iota(jnp.int32, (8, 128), 0) == 0
-    line = jnp.where(lane == 2 * t, even[...], jnp.where(lane == 2 * t + 1, odd[...], 0.0))
-    line = jnp.where(top, line, 0.0)
+        line = jnp.where(lane == 4 * b + k, charge[k].astype(f32) / charge_unit, line)
+    for k in range(4):
+        charges[k] = line
+
+
+def pack_body(field, shifted, charges, out):
+    line = jnp.sum(charges[...], axis=0)
     for c in range(4):
         for part in range(2):
-            piece = shifted[part, c] if c < 2 else field[part, c - 2]
+            piece = shifted[part, c + 2] if c < 2 else field[part, c - 2]
             for half in range(2):
                 at = (part * 2 + half) * 16
                 for r in range(4):
                     out[4 * r + c, at : at + 16, :] = piece[:, half * 128 : (half + 1) * 128]
-    for t2 in range(TRANS):
-        out[t2, 64:72, :] = line
+    for t in range(TRANS):
+        out[t, 64:72, :] = line
 
 
 def whole_field(x, part):
@@ -198,9 +201,8 @@
     take = lambda slot: chosen(own, received, slot, c < 2)
     fr, fi = whole_field(x, 0), whole_field(x, 1)
     probe(fr, fi, take(2), take(3), re, im)
-    charges = jnp.sum(x[:, 64:72, :], axis=0)
-    charges = jnp.sum(charges, axis=0, keepdims=True)
-    source = (4 * b + lax.broadcasted_iota(jnp.int32, (8, 128), 1)) % SLICES
+    charges = jnp.max(x[:, 64:72, :], axis=0)
+    source = lax.broadcasted_iota(jnp.int32, (8, 128), 1)
     pole = lax.broadcasted_iota(jnp.int32, (8, 128), 0)
     rates, freqs, amps = (jnp.zeros((8, 128), f32) for _ in range(3))
     for k in range(8):
@@ -290,18 +292,20 @@
                     target[c : c + 1, begin : begin + 256] = piece[q : q + 1]
 
 
-def call(body, outs, *args, scalars=(), scratch=()):
-    specs = [
-        pl.BlockSpec(memory_space=pltpu.SMEM if k in scalars else pltpu.VMEM)
-        for k in range(len(args))
-    ]
+def call(body, outs, *args, scalars=(), plain=(), last=False):
+    specs, inputs = [], []
+    for k, arg in enumerate(args):
+        specs.append(pl.BlockSpec(memory_space=pltpu.SMEM if k in scalars else pltpu.VMEM))
+        if k not in scalars and k not in plain:
+            arg = pltpu.with_memory_space_constraint(arg, pltpu.VMEM)
+        inputs.append(arg)
+    kind = jax.ShapeDtypeStruct if last else pltpu.VMEM
     return pl.pallas_call(
         body,
-        out_shape=[jax.ShapeDtypeStruct(shape, f32) for shape in outs],
+        out_shape=[kind(shape, f32) for shape in outs],
         in_specs=specs,
         out_specs=[pl.BlockSpec(memory_space=pltpu.VMEM) for _ in outs],
-        scratch_shapes=list(scratch),
-    )(*args)
+    )(*inputs)
 
 
 def shards(
@@ -312,17 +316,16 @@
     kept = (8, ROWS, WIDE)
     state_shape = (2, ROWS, WIDE)
     line = (ROWS, WIDE)
-    field_send, send, own, charges = call(
+    shifted = lax.ppermute(field_in, "beam", NEXT_BEAM)
+    send, own, charges = call(
         prep_body,
-        [(2, 2, 16, GRID), kept, kept, (8, 128)],
-        field_in, phases, energy, row_cell, col_cell, weight, charge,
-        scalars=(6,),
-    )
-    shifted = lax.ppermute(field_send, "beam", NEXT_BEAM)
-    even = lax.ppermute(charges, JOINT, FROM_EVEN)
-    odd = lax.ppermute(charges, JOINT, FROM_ODD)
-    received = lax.ppermute(send, JOINT, NEXT_BEAM_PAIR)
-    (packed,) = call(pack_body, [(TRANS, 72, 128)], field_in, shifted, even, odd)
+        [kept, kept, (4, 8, 128)],
+        phases, energy, row_cell, col_cell, weight, charge,
+        scalars=(5,), plain=range(5),
+    )
+    charges = lax.all_to_all(charges, JOINT, 0, 0, tiled=True, axis_index_groups=FOURS)
+    received = lax.ppermute(send, JOINT, PAIR_TO_NEXT)
+    (packed,) = call(pack_body, [(TRANS, 72, 128)], field_in, shifted, charges, plain=(0,))
     x = lax.all_to_all(packed, "trans", 0, 0, tiled=True)
     states, extra, _, _ = call(
         first_body,
@@ -334,18 +337,18 @@
     field, re, im = call(
         second_body,
         [(2, GRID, GRID), line, line],
-        x, states, own, received, extra, high, low,
+        x, states, own, received, extra, high, low, plain=(5, 6),
     )
     (final,) = call(third_body, [state_shape], following, extra, re, im)
     home = lax.ppermute(final, JOINT, TO_PREVIOUS)
     (bands,) = call(
-        fourth_body, [(4, 32, GRID)], field, final, own, received, extra, high, low
+        fourth_body, [(4, 32, GRID)], field, final, own, received, extra, high, low, plain=(5, 6)
     )
     home = jnp.concatenate([home[..., :256], home[..., 256:]], axis=1).reshape(32, 256)
     both = jnp.concatenate([bands, jnp.broadcast_to(home[None], (4, 32, 256))], axis=1)
     y = lax.all_to_all(both, "trans", 0, 0, tiled=True, axis_index_groups=QUADS)
     return tuple(
-        call(last_body, [(2, 4, 16, GRID), (4, NPART), (4, NPART)], y)
+        call(last_body, [(2, 4, 16, GRID), (4, NPART), (4, NPART)], y, last=True)
     )
 
 

time: 91.5 us -> 82.7 us (0.904)
  blocking collectives: 8.52 us -> 19.4 us
  starting transfers between devices: 37.7 us -> 28.6 us
  Pallas kernels: 21.9 us -> 16.3 us
  local copies, waits for them, and re-layouts: 3.54 us -> 0.02 us
  waiting for transfers between devices: 18.5 us -> 17.1 us
    all_to_all x0 -> x1, blocking collectives: none -> 11.5 us  [shards(): lax.all_to_all(charges, JOINT, 0, 0, tiled=True, axis_index_groups=FOURS)]
    ppermute x4 -> x2, starting transfers between devices: 16.1 us -> 5.85 us  [the longest x1 3.94 us: shards(): shifted = lax.ppermute(field_in, 'beam', NEXT_BEAM)]
    pallas_call x7, Pallas kernels: 21.9 us -> 16.3 us  [call(): pl.pallas_call(body, out_shape=[kind(shape, f32) for shape in outs], in_s...]
    unnamed x16 -> x0, local copies, waits for them, and re-layouts: 3.52 us -> none
    ppermute x4 -> x2, waiting for transfers between devices: 10.1 us -> 8.23 us  [the longest x1 8.23 us: shards(): received = lax.ppermute(send, JOINT, PAIR_TO_NEXT)]
    all_to_all x1, starting transfers between devices: 17.7 us -> 18.9 us  [shards(): x = lax.all_to_all(packed, 'trans', 0, 0, tiled=True)]
  transfers between devices with their start and end apart: 7 -> 5, of which waited for: 3 -> 3; matrix products, arithmetic and copies ran while one was open for 0% -> 0% of each run, Pallas kernels for 12% -> 13%
where the time goes in v2:
time: 82.7 us; the launch traced here: 82.2 us
  starting transfers between devices  28.6 us (35%)
  blocking collectives  19.4 us (23%)
  waiting for transfers between devices  17.1 us (21%)
  Pallas kernels  16.3 us (20%)
    all_to_all x1, starting transfers between devices, shards(): x = lax.all_to_all(packed, 'trans', 0, 0, tiled=True)  18.9 us
    pallas_call x7, Pallas kernels, call(): pl.pallas_call(body, out_shape=[kind(shape, f32) for shape in outs], in_s...  16.3 us
    all_to_all x1, blocking collectives, shards(): lax.all_to_all(charges, JOINT, 0, 0, tiled=True, axis_index_groups=FOURS)  11.5 us
    all_to_all x1, waiting for transfers between devices, shards(): x = lax.all_to_all(packed, 'trans', 0, 0, tiled=True)  8.39 us
    ppermute x1, waiting for transfers between devices, shards(): received = lax.ppermute(send, JOINT, PAIR_TO_NEXT)  8.23 us
    all_to_all x1, blocking collectives, shards(): y = lax.all_to_all(both, 'trans', 0, 0, tiled=True, axis_index_groups=QUADS)  7.86 us
    ppermute x1, starting transfers between devices, shards(): shifted = lax.ppermute(field_in, 'beam', NEXT_BEAM)  3.94 us
    ppermute x1, starting transfers between devices, shards(): home = lax.ppermute(final, JOINT, TO_PREVIOUS)  1.92 us
  transfers between devices with their start and end apart: 5, of which 3 were waited for; matrix products, arithmetic and copies ran while one was open for 0% of the time, Pallas kernels for 13%

profile of v2, /device:TPU:1, one launch (start us, length us, event | category | flops | bytes accessed | tf_op | source)
XLA Modules:
  0.0 82.2 jit_solution(10580434439246904598)
XLA Ops:
  0.6 3.9 %collective-permute-start = (f32[2,4,16,256]{3,2,1,0:T(8,128)}, f32[2,4,16,256]{3,2,1,0:T(8,128)S(1)}, u32[]{:S(2)}, u32[]{:S(2)}) collective-permute-start(f32[2,4,16,256]{3,2,1,0:T(8,128)} %field.1), channel_id=1, source_target_pairs={{0,16},{16,32},{32,48},{48,64},{64,80},{80,96},{96,112},{112,128},... | collective-permute-start | bytes 393224 | tf_op jit(solution)/shard_map/ppermute | solution.py:319
  4.6 1.0 %shard_map.139 = (f32[8,8,512]{2,1,0:T(8,128)S(1)}, f32[8,8,512]{2,1,0:T(8,128)S(1)}, f32[4,8,128]{2,1,0:T(8,128)S(1)}) custom-call(f32[4,4096]{1,0:T(4,128)} %phases.1, f32[4,4096]{1,0:T(4,128)} %energy.1, s32[4,4096]{1,0:T(4,128)} %row.1, s32[4,4096]{1,0:T(4,128)} %col.1, s32[4,4096]{1,0:T(4,128)} %weight.1, s32[4]{0:T(128)} %charge.1), custom_call_target="tpu_custom_call" | custom-call | tf_op jit(solution)/shard_map/pallas_call | solution.py:303
  5.6 11.5 %all_to_all.15.charges = f32[4,8,128]{2,1,0:T(8,128)S(1)} all-to-all(f32[4,8,128]{2,1,0:T(8,128)S(1)} %get-tuple-element.11), channel_id=1, replica_groups={{0,16,64,80},{32,48,96,112},{128,144,192,208},{160,176,224,240},{256,27..., dimensions={0} | all-to-all | bytes 32768 | tf_op jit(solution)/shard_map/all_to_all | solution.py:326
  17.2 0.0 collective-permute-done.shifted
  17.2 1.8 %shard_map.140 = f32[16,72,128]{2,1,0:T(8,128)} custom-call(f32[2,4,16,256]{3,2,1,0:T(8,128)} %field.1, f32[2,4,16,256]{3,2,1,0:T(8,128)S(1)} %collective-permute-done.shifted, f32[4,8,128]{2,1,0:T(8,128)S(1)} %all_to_all.15.charges), custom_call_target="tpu_custom_call" | custom-call | tf_op jit(solution)/shard_map/pallas_call | solution.py:303
  18.9 18.9 %all-to-all-start.1 = ((f32[16,72,128]{2,1,0:T(8,128)}), f32[16,72,128]{2,1,0:T(8,128)S(1)}, u32[]{:S(2)}, u32[]{:S(2)}) async-start(f32[16,72,128]{2,1,0:T(8,128)} %shard_map.140), calls=%async_computation.1 | async-start | bytes 1179648 | tf_op jit(solution)/shard_map/all_to_all | solution.py:329
  37.9 1.9 %collective-permute-start.1 = (f32[8,8,512]{2,1,0:T(8,128)S(1)}, f32[8,8,512]{2,1,0:T(8,128)S(1)}, u32[]{:S(2)}, u32[]{:S(2)}) collective-permute-start(f32[8,8,512]{2,1,0:T(8,128)S(1)} %get-tuple-element.13), channel_id=1, source_target_pairs={{0,16},{1,17},{4,20},{5,21},{8,24},{9,25},{12,28},{13,29},{16,32},... | collective-permute-start | bytes 393224 | tf_op jit(solution)/shard_map/ppermute | solution.py:327
  39.8 8.2 %collective-permute-done.1.received = f32[8,8,512]{2,1,0:T(8,128)S(1)} collective-permute-done((f32[8,8,512]{2,1,0:T(8,128)S(1)}, f32[8,8,512]{2,1,0:T(8,128)S(1)}, u32[]{:S(2)}, u32[]{:S(2)}) %collective-permute-start.1) | collective-permute-done | bytes 131104 | tf_op jit(solution)/shard_map/ppermute | solution.py:327
  48.0 8.4 %all-to-all-done.1.x = f32[16,72,128]{2,1,0:T(8,128)S(1)} async-done(((f32[16,72,128]{2,1,0:T(8,128)}), f32[16,72,128]{2,1,0:T(8,128)S(1)}, u32[]{:S(2)}, u32[]{:S(2)}) %all-to-all-start.1) | async-done | bytes 589856 | tf_op jit(solution)/shard_map/all_to_all | solution.py:329
  56.4 3.3 %shard_map.141 = (f32[2,8,512]{2,1,0:T(8,128)S(1)}, f32[4,8,128]{2,1,0:T(8,128)S(1)}, f32[8,512]{1,0:T(8,128)}, f32[8,512]{1,0:T(8,128)}) custom-call(f32[16,72,128]{2,1,0:T(8,128)S(1)} %all-to-all-done.1.x, f32[8,8,512]{2,1,0:T(8,128)S(1)} %get-tuple-element.12.own, f32[8,8,512]{2,1,0:T(8,128)S(1)} %collective-permute-done.1.received, f32[8]{0:T(128)} %rate.1, ...), custom_call_target="tpu_custom_call" | custom-call | tf_op jit(solution)/shard_map/pallas_call | solution.py:303
  59.7 1.9 %collective-permute-start.2 = (f32[2,8,512]{2,1,0:T(8,128)S(1)}, f32[2,8,512]{2,1,0:T(8,128)S(1)}, u32[]{:S(2)}, u32[]{:S(2)}) collective-permute-start(f32[2,8,512]{2,1,0:T(8,128)S(1)} %get-tuple-element.14.states), channel_id=1, source_target_pairs={{0,499},{1,0},{2,1},{3,2},{4,503},{5,4},{6,5},{7,6},{8,507},{9,8},... | collective-permute-start | bytes 98312 | tf_op jit(solution)/shard_map/ppermute | solution.py:336
  61.7 6.5 %shard_map.142 = (f32[2,256,256]{2,1,0:T(8,128)S(1)}, f32[8,512]{1,0:T(8,128)S(1)}, f32[8,512]{1,0:T(8,128)S(1)}) custom-call(f32[16,72,128]{2,1,0:T(8,128)S(1)} %all-to-all-done.1.x, f32[2,8,512]{2,1,0:T(8,128)S(1)} %get-tuple-element.14.states, f32[8,8,512]{2,1,0:T(8,128)S(1)} %get-tuple-element.12.own, f32[8,8,512]{2,1,0:T(8,128)S(1)} %collective-permute-done.1.received, ...), custom_call_target="tpu_custom_call" | custom-call | tf_op jit(solution)/shard_map/pallas_call | solution.py:303
  68.2 0.0 collective-permute-done.2.states
  68.2 0.1 shard_map.143.states
  68.3 1.9 %collective-permute-start.3 = (f32[2,8,512]{2,1,0:T(8,128)S(1)}, f32[2,8,512]{2,1,0:T(8,128)S(1)}, u32[]{:S(2)}, u32[]{:S(2)}) collective-permute-start(f32[2,8,512]{2,1,0:T(8,128)S(1)} %shard_map.143.states), channel_id=1, source_target_pairs={{0,499},{1,0},{2,1},{3,2},{4,503},{5,4},{6,5},{7,6},{8,507},{9,8},... | collective-permute-start | bytes 98312 | tf_op jit(solution)/shard_map/ppermute | solution.py:343
  70.2 2.9 %shard_map.144 = f32[4,32,256]{2,1,0:T(8,128)S(1)} custom-call(f32[2,256,256]{2,1,0:T(8,128)S(1)} %get-tuple-element.16.field, f32[2,8,512]{2,1,0:T(8,128)S(1)} %shard_map.143.states, f32[8,8,512]{2,1,0:T(8,128)S(1)} %get-tuple-element.12.own, f32[8,8,512]{2,1,0:T(8,128)S(1)} %collective-permute-done.1.received, f32[4,8,128]{2,1,0:T(8,128)S(1)} %get-tuple-element.15.extra, ...), custom_call_target="tpu_custom_call" | custom-call | tf_op jit(solution)/shard_map/pallas_call | solution.py:303
  73.1 0.4 collective-permute-done.3
  73.6 7.9 %all_to_all.16.x = f32[4,64,256]{2,1,0:T(8,128)S(1)} all-to-all(f32[4,64,256]{2,1,0:T(8,128)S(1)} %pad_maximum_fusion), channel_id=1, replica_groups={{0,1,2,3},{4,5,6,7},{8,9,10,11},{12,13,14,15},{16,17,18,19},{20,21,22,2..., dimensions={0} | all-to-all | bytes 524288 | tf_op jit(solution)/shard_map/all_to_all | solution.py:349
  81.4 0.7 shard_map.145
  (4 shorter events, 0.0 us)
Async XLA Ops:
  0.6 16.5 %collective-permute-start = (f32[2,4,16,256]{3,2,1,0:T(8,128)}, f32[2,4,16,256]{3,2,1,0:T(8,128)S(1)}, u32[]{:S(2)}, u32[]{:S(2)}) collective-permute-start(f32[2,4,16,256]{3,2,1,0:T(8,128)} %field.1), channel_id=1, source_target_pairs={{0,16},{16,32},{32,48},{48,64},{64,80},{80,96},{96,112},{112,128},... | collective-permute-start | bytes 393224 | tf_op jit(solution)/shard_map/ppermute | solution.py:319
  18.9 37.5 %all-to-all-start.1 = ((f32[16,72,128]{2,1,0:T(8,128)}), f32[16,72,128]{2,1,0:T(8,128)S(1)}, u32[]{:S(2)}, u32[]{:S(2)}) async-start(f32[16,72,128]{2,1,0:T(8,128)} %shard_map.140), calls=%async_computation.1 | async-start | bytes 1179648 | tf_op jit(solution)/shard_map/all_to_all | solution.py:329
  37.9 10.1 %collective-permute-start.1 = (f32[8,8,512]{2,1,0:T(8,128)S(1)}, f32[8,8,512]{2,1,0:T(8,128)S(1)}, u32[]{:S(2)}, u32[]{:S(2)}) collective-permute-start(f32[8,8,512]{2,1,0:T(8,128)S(1)} %get-tuple-element.13), channel_id=1, source_target_pairs={{0,16},{1,17},{4,20},{5,21},{8,24},{9,25},{12,28},{13,29},{16,32},... | collective-permute-start | bytes 393224 | tf_op jit(solution)/shard_map/ppermute | solution.py:327
  59.7 8.5 %collective-permute-start.2 = (f32[2,8,512]{2,1,0:T(8,128)S(1)}, f32[2,8,512]{2,1,0:T(8,128)S(1)}, u32[]{:S(2)}, u32[]{:S(2)}) collective-permute-start(f32[2,8,512]{2,1,0:T(8,128)S(1)} %get-tuple-element.14.states), channel_id=1, source_target_pairs={{0,499},{1,0},{2,1},{3,2},{4,503},{5,4},{6,5},{7,6},{8,507},{9,8},... | collective-permute-start | bytes 98312 | tf_op jit(solution)/shard_map/ppermute | solution.py:336
  68.3 5.2 %collective-permute-start.3 = (f32[2,8,512]{2,1,0:T(8,128)S(1)}, f32[2,8,512]{2,1,0:T(8,128)S(1)}, u32[]{:S(2)}, u32[]{:S(2)}) collective-permute-start(f32[2,8,512]{2,1,0:T(8,128)S(1)} %shard_map.143.states), channel_id=1, source_target_pairs={{0,499},{1,0},{2,1},{3,2},{4,503},{5,4},{6,5},{7,6},{8,507},{9,8},... | collective-permute-start | bytes 98312 | tf_op jit(solution)/shard_map/ppermute | solution.py:343

commit v3 on v2

--- a/solution.py
+++ b/solution.py
@@ -325,6 +325,7 @@
     )
     charges = lax.all_to_all(charges, JOINT, 0, 0, tiled=True, axis_index_groups=FOURS)
     received = lax.ppermute(send, JOINT, PAIR_TO_NEXT)
+    shifted, charges, received = lax.optimization_barrier((shifted, charges, received))
     (packed,) = call(pack_body, [(TRANS, 72, 128)], field_in, shifted, charges, plain=(0,))
     x = lax.all_to_all(packed, "trans", 0, 0, tiled=True)
     states, extra, _, _ = call(

time: 82.7 us -> 85.9 us (1.039)
  blocking collectives: 19.4 us -> 56.9 us
  waiting for transfers between devices: 17.1 us -> 0.01 us
  starting transfers between devices: 28.6 us -> 12.2 us
    all_to_all x0 -> x1, blocking collectives: none -> 37.1 us  [shards(): x = lax.all_to_all(packed, 'trans', 0, 0, tiled=True)]
    all_to_all x1 -> x0, starting transfers between devices: 18.9 us -> none  [shards(): x = lax.all_to_all(packed, 'trans', 0, 0, tiled=True)]
    all_to_all x1 -> x0, waiting for transfers between devices: 8.39 us -> none  [shards(): x = lax.all_to_all(packed, 'trans', 0, 0, tiled=True)]
    ppermute x1, waiting for transfers between devices: 8.23 us -> 0.01 us  [shards(): received = lax.ppermute(send, JOINT, PAIR_TO_NEXT)]
    ppermute x1, starting transfers between devices: 1.92 us -> 3.14 us  [shards(): home = lax.ppermute(final, JOINT, TO_PREVIOUS)]
    ppermute x1, starting transfers between devices: 1.91 us -> 3.12 us  [shards(): received = lax.ppermute(send, JOINT, PAIR_TO_NEXT)]
  transfers between devices with their start and end apart: 5 -> 4, of which waited for: 3 -> 0; matrix products, arithmetic and copies ran while one was open for 0% -> 0% of each run, Pallas kernels for 13% -> 12%
where the time goes in v3:
time: 85.9 us; the launch traced here: 85.5 us
  blocking collectives  56.9 us (66%)
  Pallas kernels  15.5 us (18%)
  starting transfers between devices  12.2 us (14%)
    all_to_all x1, blocking collectives, shards(): x = lax.all_to_all(packed, 'trans', 0, 0, tiled=True)  37.1 us
    pallas_call x7, Pallas kernels, call(): pl.pallas_call(body, out_shape=[kind(shape, f32) for shape in outs], in_s...  15.5 us
    all_to_all x1, blocking collectives, shards(): lax.all_to_all(charges, JOINT, 0, 0, tiled=True, axis_index_groups=FOURS)  11.5 us
    all_to_all x1, blocking collectives, shards(): y = lax.all_to_all(both, 'trans', 0, 0, tiled=True, axis_index_groups=QUADS)  8.34 us
    ppermute x1, starting transfers between devices, shards(): shifted = lax.ppermute(field_in, 'beam', NEXT_BEAM)  3.94 us
    ppermute x1, starting transfers between devices, shards(): home = lax.ppermute(final, JOINT, TO_PREVIOUS)  3.14 us
    ppermute x1, starting transfers between devices, shards(): received = lax.ppermute(send, JOINT, PAIR_TO_NEXT)  3.12 us
    ppermute x1, starting transfers between devices, shards(): following = lax.ppermute(states, JOINT, TO_PREVIOUS)  2.02 us
  transfers between devices with their start and end apart: 4, of which 0 were waited for; matrix products, arithmetic and copies ran while one was open for 0% of the time, Pallas kernels for 12%

profile of v3, /device:TPU:1, one launch (start us, length us, event | category | flops | bytes accessed | tf_op | source)
XLA Modules:
  0.0 85.5 jit_solution(369326585307490786)
XLA Ops:
  0.6 3.9 %collective-permute-start = (f32[2,4,16,256]{3,2,1,0:T(8,128)}, f32[2,4,16,256]{3,2,1,0:T(8,128)S(1)}, u32[]{:S(2)}, u32[]{:S(2)}) collective-permute-start(f32[2,4,16,256]{3,2,1,0:T(8,128)} %field.1), channel_id=1, source_target_pairs={{0,16},{16,32},{32,48},{48,64},{64,80},{80,96},{96,112},{112,128},... | collective-permute-start | bytes 393224 | tf_op jit(solution)/shard_map/ppermute | solution.py:319
  4.6 1.0 %shard_map.139 = (f32[8,8,512]{2,1,0:T(8,128)S(1)}, f32[8,8,512]{2,1,0:T(8,128)S(1)}, f32[4,8,128]{2,1,0:T(8,128)S(1)}) custom-call(f32[4,4096]{1,0:T(4,128)} %phases.1, f32[4,4096]{1,0:T(4,128)} %energy.1, s32[4,4096]{1,0:T(4,128)} %row.1, s32[4,4096]{1,0:T(4,128)} %col.1, s32[4,4096]{1,0:T(4,128)} %weight.1, s32[4]{0:T(128)} %charge.1), custom_call_target="tpu_custom_call" | custom-call | tf_op jit(solution)/shard_map/pallas_call | solution.py:303
  5.6 3.1 %collective-permute-start.1 = (f32[8,8,512]{2,1,0:T(8,128)S(1)}, f32[8,8,512]{2,1,0:T(8,128)S(1)}, u32[]{:S(2)}, u32[]{:S(2)}) collective-permute-start(f32[8,8,512]{2,1,0:T(8,128)S(1)} %get-tuple-element.15), channel_id=1, source_target_pairs={{0,16},{1,17},{4,20},{5,21},{8,24},{9,25},{12,28},{13,29},{16,32},... | collective-permute-start | bytes 393224 | tf_op jit(solution)/shard_map/ppermute | solution.py:327
  8.8 11.5 %all_to_all.15.charges = f32[4,8,128]{2,1,0:T(8,128)S(1)} all-to-all(f32[4,8,128]{2,1,0:T(8,128)S(1)} %get-tuple-element.14), channel_id=1, replica_groups={{0,16,64,80},{32,48,96,112},{128,144,192,208},{160,176,224,240},{256,27..., dimensions={0} | all-to-all | bytes 32768 | tf_op jit(solution)/shard_map/all_to_all | solution.py:326
  20.2 0.0 collective-permute-done.shifted
  20.2 0.0 collective-permute-done.1.received
  20.2 0.9 %shard_map.140 = f32[16,72,128]{2,1,0:T(8,128)S(1)} custom-call(f32[2,4,16,256]{3,2,1,0:T(8,128)} %field.1, f32[2,4,16,256]{3,2,1,0:T(8,128)S(1)} %collective-permute-done.shifted, f32[4,8,128]{2,1,0:T(8,128)S(1)} %all_to_all.15.charges), custom_call_target="tpu_custom_call" | custom-call | tf_op jit(solution)/shard_map/pallas_call | solution.py:303
  21.2 37.1 %all_to_all.16.x = f32[16,72,128]{2,1,0:T(8,128)S(1)} all-to-all(f32[16,72,128]{2,1,0:T(8,128)S(1)} %shard_map.140), channel_id=1, replica_groups=mesh['beam'=32,'trans'=16] {'trans'}, dimensions={0} | all-to-all | bytes 1179648 | tf_op jit(solution)/shard_map/all_to_all | solution.py:330
  58.3 3.3 %shard_map.141 = (f32[2,8,512]{2,1,0:T(8,128)S(1)}, f32[4,8,128]{2,1,0:T(8,128)S(1)}, f32[8,512]{1,0:T(8,128)}, f32[8,512]{1,0:T(8,128)}) custom-call(f32[16,72,128]{2,1,0:T(8,128)S(1)} %all_to_all.16.x, f32[8,8,512]{2,1,0:T(8,128)S(1)} %get-tuple-element.18.own, f32[8,8,512]{2,1,0:T(8,128)S(1)} %collective-permute-done.1.received, f32[8]{0:T(128)} %rate.1, ...), custom_call_target="tpu_custom_call" | custom-call | tf_op jit(solution)/shard_map/pallas_call | solution.py:303
  61.6 2.0 %collective-permute-start.2 = (f32[2,8,512]{2,1,0:T(8,128)S(1)}, f32[2,8,512]{2,1,0:T(8,128)S(1)}, u32[]{:S(2)}, u32[]{:S(2)}) collective-permute-start(f32[2,8,512]{2,1,0:T(8,128)S(1)} %get-tuple-element.20.states), channel_id=1, source_target_pairs={{0,499},{1,0},{2,1},{3,2},{4,503},{5,4},{6,5},{7,6},{8,507},{9,8},... | collective-permute-start | bytes 98312 | tf_op jit(solution)/shard_map/ppermute | solution.py:337
  63.7 6.5 %shard_map.142 = (f32[2,256,256]{2,1,0:T(8,128)S(1)}, f32[8,512]{1,0:T(8,128)S(1)}, f32[8,512]{1,0:T(8,128)S(1)}) custom-call(f32[16,72,128]{2,1,0:T(8,128)S(1)} %all_to_all.16.x, f32[2,8,512]{2,1,0:T(8,128)S(1)} %get-tuple-element.20.states, f32[8,8,512]{2,1,0:T(8,128)S(1)} %get-tuple-element.18.own, f32[8,8,512]{2,1,0:T(8,128)S(1)} %collective-permute-done.1.received, ...), custom_call_target="tpu_custom_call" | custom-call | tf_op jit(solution)/shard_map/pallas_call | solution.py:303
  70.2 0.0 collective-permute-done.2.states
  70.2 0.1 shard_map.143.states
  70.3 3.1 %collective-permute-start.3 = (f32[2,8,512]{2,1,0:T(8,128)S(1)}, f32[2,8,512]{2,1,0:T(8,128)S(1)}, u32[]{:S(2)}, u32[]{:S(2)}) collective-permute-start(f32[2,8,512]{2,1,0:T(8,128)S(1)} %shard_map.143.states), channel_id=1, source_target_pairs={{0,499},{1,0},{2,1},{3,2},{4,503},{5,4},{6,5},{7,6},{8,507},{9,8},... | collective-permute-start | bytes 98312 | tf_op jit(solution)/shard_map/ppermute | solution.py:344
  73.4 2.9 %shard_map.144 = f32[4,32,256]{2,1,0:T(8,128)S(1)} custom-call(f32[2,256,256]{2,1,0:T(8,128)S(1)} %get-tuple-element.22.field, f32[2,8,512]{2,1,0:T(8,128)S(1)} %shard_map.143.states, f32[8,8,512]{2,1,0:T(8,128)S(1)} %get-tuple-element.18.own, f32[8,8,512]{2,1,0:T(8,128)S(1)} %collective-permute-done.1.received, f32[4,8,128]{2,1,0:T(8,128)S(1)} %get-tuple-element.21.extra, ...), custom_call_target="tpu_custom_call" | custom-call | tf_op jit(solution)/shard_map/pallas_call | solution.py:303
  76.3 0.0 collective-permute-done.3
  76.4 8.3 %all_to_all.17.x = f32[4,64,256]{2,1,0:T(8,128)S(1)} all-to-all(f32[4,64,256]{2,1,0:T(8,128)S(1)} %pad_maximum_fusion), channel_id=1, replica_groups={{0,1,2,3},{4,5,6,7},{8,9,10,11},{12,13,14,15},{16,17,18,19},{20,21,22,2..., dimensions={0} | all-to-all | bytes 524288 | tf_op jit(solution)/shard_map/all_to_all | solution.py:350
  84.7 0.7 shard_map.145
  (4 shorter events, 0.0 us)
Async XLA Ops:
  0.6 19.6 %collective-permute-start = (f32[2,4,16,256]{3,2,1,0:T(8,128)}, f32[2,4,16,256]{3,2,1,0:T(8,128)S(1)}, u32[]{:S(2)}, u32[]{:S(2)}) collective-permute-start(f32[2,4,16,256]{3,2,1,0:T(8,128)} %field.1), channel_id=1, source_target_pairs={{0,16},{16,32},{32,48},{48,64},{64,80},{80,96},{96,112},{112,128},... | collective-permute-start | bytes 393224 | tf_op jit(solution)/shard_map/ppermute | solution.py:319
  5.6 14.6 %collective-permute-start.1 = (f32[8,8,512]{2,1,0:T(8,128)S(1)}, f32[8,8,512]{2,1,0:T(8,128)S(1)}, u32[]{:S(2)}, u32[]{:S(2)}) collective-permute-start(f32[8,8,512]{2,1,0:T(8,128)S(1)} %get-tuple-element.15), channel_id=1, source_target_pairs={{0,16},{1,17},{4,20},{5,21},{8,24},{9,25},{12,28},{13,29},{16,32},... | collective-permute-start | bytes 393224 | tf_op jit(solution)/shard_map/ppermute | solution.py:327
  61.6 8.6 %collective-permute-start.2 = (f32[2,8,512]{2,1,0:T(8,128)S(1)}, f32[2,8,512]{2,1,0:T(8,128)S(1)}, u32[]{:S(2)}, u32[]{:S(2)}) collective-permute-start(f32[2,8,512]{2,1,0:T(8,128)S(1)} %get-tuple-element.20.states), channel_id=1, source_target_pairs={{0,499},{1,0},{2,1},{3,2},{4,503},{5,4},{6,5},{7,6},{8,507},{9,8},... | collective-permute-start | bytes 98312 | tf_op jit(solution)/shard_map/ppermute | solution.py:337
  70.3 6.0 %collective-permute-start.3 = (f32[2,8,512]{2,1,0:T(8,128)S(1)}, f32[2,8,512]{2,1,0:T(8,128)S(1)}, u32[]{:S(2)}, u32[]{:S(2)}) collective-permute-start(f32[2,8,512]{2,1,0:T(8,128)S(1)} %shard_map.143.states), channel_id=1, source_target_pairs={{0,499},{1,0},{2,1},{3,2},{4,503},{5,4},{6,5},{7,6},{8,507},{9,8},... | collective-permute-start | bytes 98312 | tf_op jit(solution)/shard_map/ppermute | solution.py:344

commit v4 on v2

--- a/solution.py
+++ b/solution.py
@@ -1,5 +1,4 @@
 import functools
-import math
 
 import jax
 import jax.numpy as jnp
@@ -51,23 +50,8 @@
     return out
 
 
-SPREAD = (
-    (1, 4, 5), (3, 8, 11), (12, 20, 24), (7, 27, 28), (9, 16, 25), (2, 21, 23),
-    (14, 19, 29), (15, 17, 30), (13, 18, 31), (6, 26, 28), (10, 22, 28),
-)
-FOURS = [
-    [m * TRANS + t for m in group]
-    for t in range(TRANS)
-    for group in sorted({tuple(sorted([b, *(b ^ v for v in SPREAD[t % 11])])) for b in range(BEAM)})
-]
 TO_PREVIOUS = moved(lambda b, t: ((4 * b + t % 4 - 1) // 4, t // 4 * 4 + (t % 4 - 1) % 4))
 NEXT_BEAM = [(b, (b + 1) % BEAM) for b in range(BEAM)]
-PAIR_TO_NEXT = [
-    (b * TRANS + t, (b + 1) % BEAM * TRANS + t)
-    for b in range(BEAM)
-    for t in range(TRANS)
-    if t % 4 < 2
-]
 
 
 def split(x):
@@ -122,17 +106,16 @@
     col_iota = iota_rows(0, GRID).astype(bf16)
     row_iota = iota_rows(LOW, SPAN).astype(bf16)
     zero = jnp.zeros((), bf16)
-    total = jnp.zeros((2 * SPAN, GRID), f32)
+    total = [jnp.zeros((SPAN, GRID), f32)] * 2
     for q in range(ROWS):
         col_hot = hot(cols[q : q + 1], col_iota)
         mask = row_iota == rows[q : q + 1].astype(bf16)
-        left = jnp.concatenate(
-            [jnp.where(mask, v[q : q + 1], zero), jnp.where(mask, u[q : q + 1], zero)], axis=0
-        )
-        total = total + lax.dot_general(
-            left, col_hot, (((1,), (1,)), ((), ())), preferred_element_type=f32
-        )
-    return total[:SPAN], total[SPAN:]
+        for k, value in enumerate((v, u)):
+            left = jnp.where(mask, value[q : q + 1], zero)
+            total[k] = total[k] + lax.dot_general(
+                left, col_hot, (((1,), (1,)), ((), ())), preferred_element_type=f32
+            )
+    return total
 
 
 def deposited(field, change, strength):
@@ -146,41 +129,49 @@
     return lax.axis_index("beam"), t, t % 4, t // 4
 
 
-def prep_body(phases, energy, row, col, weight, charge, send, own, charges):
-    b, _, c, _ = place()
-    one, two = jnp.where(c == 0, 2, 3), 3
+def prep_body(field, phases, energy, row, col, weight, send, own):
+    _, _, c, _ = place()
+    for part in range(2):
+        for k in range(2):
+            send[part * 2 + k] = field[part, 2 + k]
     own_one, own_two = jnp.maximum(c - 2, 0), jnp.maximum(c - 1, 0)
 
-    def pick(ref, index, target, slot):
+    def pick(ref, index, slot):
         line = ref[pl.ds(index, 1), :].astype(f32)
         for q in range(ROWS):
-            target[slot, q : q + 1, :] = line[:, q * WIDE : (q + 1) * WIDE]
+            own[slot, q : q + 1, :] = line[:, q * WIDE : (q + 1) * WIDE]
 
     for slot, ref in enumerate((phases, energy, row, col, weight)):
-        pick(ref, one, send, slot)
-        pick(ref, own_one, own, slot)
+        pick(ref, own_one, slot)
+        for k in range(2):
+            line = ref[2 + k : 3 + k, :].astype(f32)
+            for q in range(ROWS):
+                for half in range(2):
+                    begin = q * WIDE + half * 256
+                    at = half * 8 + q
+                    send[4 + 2 * slot + k, at : at + 1, :] = line[:, begin : begin + 256]
     for slot, ref in enumerate((row, col, weight)):
-        pick(ref, two, send, 5 + slot)
-        pick(ref, own_two, own, 5 + slot)
+        pick(ref, own_two, 5 + slot)
+
+
+def line_body(charge, charges):
+    b, _, _, _ = place()
     lane = lax.broadcasted_iota(jnp.int32, (8, 128), 1)
     line = jnp.zeros((8, 128), f32)
     for k in range(4):
         line = jnp.where(lane == 4 * b + k, charge[k].astype(f32) / charge_unit, line)
-    for k in range(4):
+    for k in range(BEAM):
         charges[k] = line
 
 
-def pack_body(field, shifted, charges, out):
-    line = jnp.sum(charges[...], axis=0)
+def pack_body(field, received, out):
     for c in range(4):
         for part in range(2):
-            piece = shifted[part, c + 2] if c < 2 else field[part, c - 2]
+            piece = received[part * 2 + c] if c < 2 else field[part, c - 2]
             for half in range(2):
                 at = (part * 2 + half) * 16
                 for r in range(4):
                     out[4 * r + c, at : at + 16, :] = piece[:, half * 128 : (half + 1) * 128]
-    for t in range(TRANS):
-        out[t, 64:72, :] = line
 
 
 def whole_field(x, part):
@@ -191,17 +182,22 @@
     return jnp.concatenate(halves, axis=1)
 
 
-def chosen(own, received, slot, from_received):
-    return jnp.where(from_received, received[slot], own[slot])
-
-
-def first_body(x, own, received, rate, freq, amp, states, extra, re, im):
+def period_one(own, received, c, slot):
+    piece = received[4 + 2 * slot + jnp.minimum(c, 1)]
+    piece = jnp.concatenate([piece[:8], piece[8:]], axis=1)
+    return jnp.where(c < 2, piece, own[slot])
+
+
+def period_two(own, received, c, slot):
+    piece = received[4 + 2 * slot + 1]
+    piece = jnp.concatenate([piece[:8], piece[8:]], axis=1)
+    return jnp.where(c < 1, piece, own[slot + 3])
+
+
+def wake_body(gathered, rate, freq, amp, extra):
     b, _, c, _ = place()
     g = 4 * b + c
-    take = lambda slot: chosen(own, received, slot, c < 2)
-    fr, fi = whole_field(x, 0), whole_field(x, 1)
-    probe(fr, fi, take(2), take(3), re, im)
-    charges = jnp.max(x[:, 64:72, :], axis=0)
+    charges = jnp.sum(gathered[...], axis=0)
     source = lax.broadcasted_iota(jnp.int32, (8, 128), 1)
     pole = lax.broadcasted_iota(jnp.int32, (8, 128), 0)
     rates, freqs, amps = (jnp.zeros((8, 128), f32) for _ in range(3))
@@ -213,19 +209,27 @@
     def total(value):
         return jnp.sum(jnp.sum(value, axis=0, keepdims=True), axis=1, keepdims=True)
 
-    wakes, norms = [], []
-    for back in (2, 1):
+    for k, back in enumerate((2, 1)):
         s = (g + SLICES - back) % SLICES
         steps = jnp.maximum(s - source, 0).astype(f32)
         power = jnp.exp(-rates * steps) * jnp.cos(freqs * steps)
         reach = jnp.where(source < s, power, jnp.where(source == s, 0.5, 0.0))
-        wakes.append(wake_gain / SLICES * total(amps * reach * charges))
-        norms.append(total(jnp.where((source == s) & (pole == 0), charges, 0.0)))
-    for k, value in enumerate((*wakes, *norms)):
-        extra[k] = jnp.broadcast_to(value, (8, 128))
+        wake = wake_gain / SLICES * total(amps * reach * charges)
+        norm = total(jnp.where((source == s) & (pole == 0), charges, 0.0))
+        extra[k] = jnp.broadcast_to(wake, (8, 128))
+        extra[2 + k] = jnp.broadcast_to(norm, (8, 128))
+
+
+def first_body(x, own, received, extra, states, re, im):
+    _, _, c, _ = place()
+    take = functools.partial(period_one, own, received, c)
+    fr, fi = whole_field(x, 0), whole_field(x, 1)
+    probe(fr, fi, take(2), take(3), re, im)
     angles = take(0)
     energies = (
-        take(1) - kick_gain * (re[...] * jnp.cos(angles) - im[...] * jnp.sin(angles)) - wakes[0]
+        take(1)
+        - kick_gain * (re[...] * jnp.cos(angles) - im[...] * jnp.sin(angles))
+        - extra[0, 0:1, 0:1]
     )
     states[0] = angles + energies
     states[1] = energies
@@ -233,7 +237,7 @@
 
 def second_body(x, states, own, received, extra, high, low, field, re, im):
     b, _, c, _ = place()
-    take = lambda slot: chosen(own, received, slot, c < 2)
+    take = functools.partial(period_one, own, received, c)
     br, bi = deposit(states[0], take(4), take(2), take(3))
     strength = deposit_gain * extra[2, 0:1, 0:1]
     fr = deposited(whole_field(x, 0), br, strength)
@@ -245,8 +249,8 @@
     fi = jnp.where(first, 0.0, fi)
     field[0] = fr
     field[1] = fi
-    take = lambda slot: chosen(own, received, slot, c < 1)
-    probe(fr, fi, take(5), take(6), re, im)
+    take = functools.partial(period_two, own, received, c)
+    probe(fr, fi, take(2), take(3), re, im)
 
 
 def third_body(states, extra, re, im, out):
@@ -262,8 +266,8 @@
 
 def fourth_body(field, states, own, received, extra, high, low, out):
     b, _, c, r = place()
-    take = lambda slot: chosen(own, received, slot, c < 1)
-    br, bi = deposit(states[0], take(7), take(5), take(6))
+    take = functools.partial(period_two, own, received, c)
+    br, bi = deposit(states[0], take(4), take(2), take(3))
     strength = deposit_gain * extra[3, 0:1, 0:1]
     fr = deposited(field[0], br, strength)
     fi = deposited(field[1], bi, strength)
@@ -316,22 +320,22 @@
     kept = (8, ROWS, WIDE)
     state_shape = (2, ROWS, WIDE)
     line = (ROWS, WIDE)
-    shifted = lax.ppermute(field_in, "beam", NEXT_BEAM)
-    send, own, charges = call(
+    send, own = call(
         prep_body,
-        [kept, kept, (4, 8, 128)],
-        phases, energy, row_cell, col_cell, weight, charge,
-        scalars=(5,), plain=range(5),
-    )
-    charges = lax.all_to_all(charges, JOINT, 0, 0, tiled=True, axis_index_groups=FOURS)
-    received = lax.ppermute(send, JOINT, PAIR_TO_NEXT)
-    (packed,) = call(pack_body, [(TRANS, 72, 128)], field_in, shifted, charges, plain=(0,))
+        [(14, 16, GRID), kept],
+        field_in, phases, energy, row_cell, col_cell, weight,
+        plain=range(6),
+    )
+    received = lax.ppermute(send, "beam", NEXT_BEAM)
+    (charges,) = call(line_body, [(BEAM, 8, 128)], charge, scalars=(0,))
+    charges = lax.all_to_all(charges, "beam", 0, 0, tiled=True)
+    (extra,) = call(
+        wake_body, [(4, 8, 128)], charges, pole_rate, pole_freq, pole_amp, scalars=(1, 2, 3)
+    )
+    (packed,) = call(pack_body, [(TRANS, 64, 128)], field_in, received, plain=(0,))
     x = lax.all_to_all(packed, "trans", 0, 0, tiled=True)
-    states, extra, _, _ = call(
-        first_body,
-        [state_shape, (4, 8, 128), line, line],
-        x, own, received, pole_rate, pole_freq, pole_amp,
-        scalars=(3, 4, 5),
+    states, _, _ = call(
+        first_body, [state_shape, line, line], x, own, received, extra
     )
     following = lax.ppermute(states, JOINT, TO_PREVIOUS)
     field, re, im = call(

time: 82.7 us -> 82.4 us (level)
  blocking collectives: 19.4 us -> 8.29 us
  waiting for transfers between devices: 17.1 us -> 25.7 us
  Pallas kernels: 16.3 us -> 18 us
    all_to_all x1 -> x0, blocking collectives: 11.5 us -> none  [shards(): lax.all_to_all(charges, JOINT, 0, 0, tiled=True, axis_index_groups=FOURS)]
    all_to_all x0 -> x1, starting transfers between devices: none -> 10.5 us  [shards(): charges = lax.all_to_all(charges, 'beam', 0, 0, tiled=True)]
    all_to_all x1, waiting for transfers between devices: 8.39 us -> 16.4 us  [shards(): x = lax.all_to_all(packed, 'trans', 0, 0, tiled=True)]
    all_to_all x1, starting transfers between devices: 18.9 us -> 11.7 us  [shards(): x = lax.all_to_all(packed, 'trans', 0, 0, tiled=True)]
    ppermute x2 -> x1, starting transfers between devices: 5.85 us -> 3.14 us  [shards(): received = lax.ppermute(send, 'beam', NEXT_BEAM)]
    pallas_call x7 -> x9, Pallas kernels: 16.3 us -> 18 us  [call(): pl.pallas_call(body, out_shape=[kind(shape, f32) for shape in outs], in_s...]
    ppermute x2 -> x1, waiting for transfers between devices: 8.23 us -> 9.2 us  [shards(): received = lax.ppermute(send, 'beam', NEXT_BEAM)]
  transfers between devices with their start and end apart: 5 -> 5, of which waited for: 3 -> 3; matrix products, arithmetic and copies ran while one was open for 0% -> 0% of each run, Pallas kernels for 13% -> 16%
where the time goes in v4:
time: 82.4 us; the launch traced here: 81.9 us
  starting transfers between devices  29.2 us (35%)
  waiting for transfers between devices  25.7 us (31%)
  Pallas kernels  18 us (22%)
  blocking collectives  8.29 us (10%)
    pallas_call x9, Pallas kernels, call(): pl.pallas_call(body, out_shape=[kind(shape, f32) for shape in outs], in_s...  18 us
    all_to_all x1, waiting for transfers between devices, shards(): x = lax.all_to_all(packed, 'trans', 0, 0, tiled=True)  16.4 us
    all_to_all x1, starting transfers between devices, shards(): x = lax.all_to_all(packed, 'trans', 0, 0, tiled=True)  11.7 us
    all_to_all x1, starting transfers between devices, shards(): charges = lax.all_to_all(charges, 'beam', 0, 0, tiled=True)  10.5 us
    ppermute x1, waiting for transfers between devices, shards(): received = lax.ppermute(send, 'beam', NEXT_BEAM)  9.2 us
    all_to_all x1, blocking collectives, shards(): y = lax.all_to_all(both, 'trans', 0, 0, tiled=True, axis_index_groups=QUADS)  8.29 us
    ppermute x1, starting transfers between devices, shards(): received = lax.ppermute(send, 'beam', NEXT_BEAM)  3.14 us
    ppermute x1, starting transfers between devices, shards(): home = lax.ppermute(final, JOINT, TO_PREVIOUS)  1.92 us
  transfers between devices with their start and end apart: 5, of which 3 were waited for; matrix products, arithmetic and copies ran while one was open for 0% of the time, Pallas kernels for 16%

profile of v4, /device:TPU:1, one launch (start us, length us, event | category | flops | bytes accessed | tf_op | source)
XLA Modules:
  0.0 81.9 jit_solution(17022384822006378826)
XLA Ops:
  0.6 1.3 %shard_map.141 = f32[32,8,128]{2,1,0:T(8,128)} custom-call(s32[4]{0:T(128)} %charge.1), custom_call_target="tpu_custom_call" | custom-call | tf_op jit(solution)/shard_map/pallas_call | solution.py:307
  2.0 10.5 %all-to-all-start.1 = ((f32[32,8,128]{2,1,0:T(8,128)}), f32[32,8,128]{2,1,0:T(8,128)S(1)}, u32[]{:S(2)}, u32[]{:S(2)}) async-start(f32[32,8,128]{2,1,0:T(8,128)} %shard_map.141), calls=%async_computation.1 | async-start | bytes 262144 | tf_op jit(solution)/shard_map/all_to_all | solution.py:331
  12.5 1.1 %shard_map.139 = (f32[14,16,256]{2,1,0:T(8,128)S(1)}, f32[8,8,512]{2,1,0:T(8,128)S(1)}) custom-call(f32[2,4,16,256]{3,2,1,0:T(8,128)} %field.3, f32[4,4096]{1,0:T(4,128)} %phases.1, f32[4,4096]{1,0:T(4,128)} %energy.1, s32[4,4096]{1,0:T(4,128)} %row.1, s32[4,4096]{1,0:T(4,128)} %col.1, s32[4,4096]{1,0:T(4,128)} %weight.1), custom_call_target="tpu_custom_call" | custom-call | tf_op jit(solution)/shard_map/pallas_call | solution.py:307
  13.6 3.1 %collective-permute-start = (f32[14,16,256]{2,1,0:T(8,128)S(1)}, f32[14,16,256]{2,1,0:T(8,128)S(1)}, u32[]{:S(2)}, u32[]{:S(2)}) collective-permute-start(f32[14,16,256]{2,1,0:T(8,128)S(1)} %get-tuple-element.9), channel_id=1, source_target_pairs={{0,16},{16,32},{32,48},{48,64},{64,80},{80,96},{96,112},{112,128},... | collective-permute-start | bytes 688136 | tf_op jit(solution)/shard_map/ppermute | solution.py:329
  16.7 9.2 %collective-permute-done.received = f32[14,16,256]{2,1,0:T(8,128)S(1)} collective-permute-done((f32[14,16,256]{2,1,0:T(8,128)S(1)}, f32[14,16,256]{2,1,0:T(8,128)S(1)}, u32[]{:S(2)}, u32[]{:S(2)}) %collective-permute-start) | collective-permute-done | bytes 229408 | tf_op jit(solution)/shard_map/ppermute | solution.py:329
  25.9 1.7 %shard_map.140 = f32[16,64,128]{2,1,0:T(8,128)} custom-call(f32[2,4,16,256]{3,2,1,0:T(8,128)} %field.3, f32[14,16,256]{2,1,0:T(8,128)S(1)} %collective-permute-done.received), custom_call_target="tpu_custom_call" | custom-call | tf_op jit(solution)/shard_map/pallas_call | solution.py:307
  27.7 0.0 all-to-all-done.1.gathered
  27.7 11.7 %all-to-all-start = ((f32[16,64,128]{2,1,0:T(8,128)}), f32[16,64,128]{2,1,0:T(8,128)S(1)}, u32[]{:S(2)}, u32[]{:S(2)}) async-start(f32[16,64,128]{2,1,0:T(8,128)} %shard_map.140), calls=%async_computation | async-start | bytes 1048576 | tf_op jit(solution)/shard_map/all_to_all | solution.py:336
  39.4 0.8 %shard_map.142.extra = f32[4,8,128]{2,1,0:T(8,128)S(1)} custom-call(f32[32,8,128]{2,1,0:T(8,128)S(1)} %all-to-all-done.1.gathered, f32[8]{0:T(128)} %rate.1, f32[8]{0:T(128)} %freq.1, f32[8]{0:T(128)} %amp.1), custom_call_target="tpu_custom_call" | custom-call | tf_op jit(solution)/shard_map/pallas_call | solution.py:307
  40.3 16.4 %all-to-all-done.x = f32[16,64,128]{2,1,0:T(8,128)S(1)} async-done(((f32[16,64,128]{2,1,0:T(8,128)}), f32[16,64,128]{2,1,0:T(8,128)S(1)}, u32[]{:S(2)}, u32[]{:S(2)}) %all-to-all-start) | async-done | bytes 524320 | tf_op jit(solution)/shard_map/all_to_all | solution.py:336
  56.6 2.7 %shard_map.143 = (f32[2,8,512]{2,1,0:T(8,128)S(1)}, f32[8,512]{1,0:T(8,128)}, f32[8,512]{1,0:T(8,128)}) custom-call(f32[16,64,128]{2,1,0:T(8,128)S(1)} %all-to-all-done.x, f32[8,8,512]{2,1,0:T(8,128)S(1)} %get-tuple-element.10.own, f32[14,16,256]{2,1,0:T(8,128)S(1)} %collective-permute-done.received, f32[4,8,128]{2,1,0:T(8,128)S(1)} %shard_map.142.extra), custom_call_target="tpu_custom_call" | custom-call | tf_op jit(solution)/shard_map/pallas_call | solution.py:307
  59.3 1.9 %collective-permute-start.1 = (f32[2,8,512]{2,1,0:T(8,128)S(1)}, f32[2,8,512]{2,1,0:T(8,128)S(1)}, u32[]{:S(2)}, u32[]{:S(2)}) collective-permute-start(f32[2,8,512]{2,1,0:T(8,128)S(1)} %get-tuple-element.11.states), channel_id=1, source_target_pairs={{0,499},{1,0},{2,1},{3,2},{4,503},{5,4},{6,5},{7,6},{8,507},{9,8},... | collective-permute-start | bytes 98312 | tf_op jit(solution)/shard_map/ppermute | solution.py:340
  61.2 6.3 %shard_map.144 = (f32[2,256,256]{2,1,0:T(8,128)S(1)}, f32[8,512]{1,0:T(8,128)S(1)}, f32[8,512]{1,0:T(8,128)S(1)}) custom-call(f32[16,64,128]{2,1,0:T(8,128)S(1)} %all-to-all-done.x, f32[2,8,512]{2,1,0:T(8,128)S(1)} %get-tuple-element.11.states, f32[8,8,512]{2,1,0:T(8,128)S(1)} %get-tuple-element.10.own, f32[14,16,256]{2,1,0:T(8,128)S(1)} %collective-permute-done.received, ...), custom_call_target="tpu_custom_call" | custom-call | tf_op jit(solution)/shard_map/pallas_call | solution.py:307
  67.5 0.0 collective-permute-done.1.states
  67.5 0.1 shard_map.145.states
  67.6 1.9 %collective-permute-start.2 = (f32[2,8,512]{2,1,0:T(8,128)S(1)}, f32[2,8,512]{2,1,0:T(8,128)S(1)}, u32[]{:S(2)}, u32[]{:S(2)}) collective-permute-start(f32[2,8,512]{2,1,0:T(8,128)S(1)} %shard_map.145.states), channel_id=1, source_target_pairs={{0,499},{1,0},{2,1},{3,2},{4,503},{5,4},{6,5},{7,6},{8,507},{9,8},... | collective-permute-start | bytes 98312 | tf_op jit(solution)/shard_map/ppermute | solution.py:347
  69.5 3.2 %shard_map.146 = f32[4,32,256]{2,1,0:T(8,128)S(1)} custom-call(f32[2,256,256]{2,1,0:T(8,128)S(1)} %get-tuple-element.12.field, f32[2,8,512]{2,1,0:T(8,128)S(1)} %shard_map.145.states, f32[8,8,512]{2,1,0:T(8,128)S(1)} %get-tuple-element.10.own, f32[14,16,256]{2,1,0:T(8,128)S(1)} %collective-permute-done.received, f32[4,8,128]{2,1,0:T(8,128)S(1)} %shard_map.142.extra, ...), custom_call_target="tpu_custom_call" | custom-call | tf_op jit(solution)/shard_map/pallas_call | solution.py:307
  72.7 0.1 collective-permute-done.2
  72.9 8.3 %all_to_all.15.x = f32[4,64,256]{2,1,0:T(8,128)S(1)} all-to-all(f32[4,64,256]{2,1,0:T(8,128)S(1)} %pad_maximum_fusion), channel_id=1, replica_groups={{0,1,2,3},{4,5,6,7},{8,9,10,11},{12,13,14,15},{16,17,18,19},{20,21,22,2..., dimensions={0} | all-to-all | bytes 524288 | tf_op jit(solution)/shard_map/all_to_all | solution.py:353
  81.1 0.7 shard_map.147
  (4 shorter events, 0.0 us)
Async XLA Ops:
  2.0 25.7 %all-to-all-start.1 = ((f32[32,8,128]{2,1,0:T(8,128)}), f32[32,8,128]{2,1,0:T(8,128)S(1)}, u32[]{:S(2)}, u32[]{:S(2)}) async-start(f32[32,8,128]{2,1,0:T(8,128)} %shard_map.141), calls=%async_computation.1 | async-start | bytes 262144 | tf_op jit(solution)/shard_map/all_to_all | solution.py:331
  13.6 12.3 %collective-permute-start = (f32[14,16,256]{2,1,0:T(8,128)S(1)}, f32[14,16,256]{2,1,0:T(8,128)S(1)}, u32[]{:S(2)}, u32[]{:S(2)}) collective-permute-start(f32[14,16,256]{2,1,0:T(8,128)S(1)} %get-tuple-element.9), channel_id=1, source_target_pairs={{0,16},{16,32},{32,48},{48,64},{64,80},{80,96},{96,112},{112,128},... | collective-permute-start | bytes 688136 | tf_op jit(solution)/shard_map/ppermute | solution.py:329
  27.7 28.9 %all-to-all-start = ((f32[16,64,128]{2,1,0:T(8,128)}), f32[16,64,128]{2,1,0:T(8,128)S(1)}, u32[]{:S(2)}, u32[]{:S(2)}) async-start(f32[16,64,128]{2,1,0:T(8,128)} %shard_map.140), calls=%async_computation | async-start | bytes 1048576 | tf_op jit(solution)/shard_map/all_to_all | solution.py:336
  59.3 8.2 %collective-permute-start.1 = (f32[2,8,512]{2,1,0:T(8,128)S(1)}, f32[2,8,512]{2,1,0:T(8,128)S(1)}, u32[]{:S(2)}, u32[]{:S(2)}) collective-permute-start(f32[2,8,512]{2,1,0:T(8,128)S(1)} %get-tuple-element.11.states), channel_id=1, source_target_pairs={{0,499},{1,0},{2,1},{3,2},{4,503},{5,4},{6,5},{7,6},{8,507},{9,8},... | collective-permute-start | bytes 98312 | tf_op jit(solution)/shard_map/ppermute | solution.py:340
  67.6 5.2 %collective-permute-start.2 = (f32[2,8,512]{2,1,0:T(8,128)S(1)}, f32[2,8,512]{2,1,0:T(8,128)S(1)}, u32[]{:S(2)}, u32[]{:S(2)}) collective-permute-start(f32[2,8,512]{2,1,0:T(8,128)S(1)} %shard_map.145.states), channel_id=1, source_target_pairs={{0,499},{1,0},{2,1},{3,2},{4,503},{5,4},{6,5},{7,6},{8,507},{9,8},... | collective-permute-start | bytes 98312 | tf_op jit(solution)/shard_map/ppermute | solution.py:347

commit v5 on v4

--- a/solution.py
+++ b/solution.py
@@ -38,7 +38,9 @@
     parts = np.stack([a.real, a.imag]).astype(np.float32)
     high = parts.astype(jnp.bfloat16)
     low = (parts - high.astype(np.float32)).astype(jnp.bfloat16)
-    return high, low
+    tall = np.stack([part.reshape(2 * GRID, GRID) for part in (high, low)])
+    wide = np.stack([np.concatenate([part[0], part[1]], axis=1) for part in (high, low)])
+    return wide, tall
 
 
 def moved(fn):
@@ -64,20 +66,21 @@
 
 
 def times_right(xr, xi, high, low):
-    m = xr.shape[0]
-    xh, xl = split(jnp.concatenate([xr, xi], axis=0))
-    pr = dot(xh, high[0]) + dot(xl, high[0]) + dot(xh, low[0])
-    pi = dot(xh, high[1]) + dot(xl, high[1]) + dot(xh, low[1])
-    return pr[:m] - pi[m:], pi[:m] + pr[m:]
+    p = []
+    for x in (xr, xi):
+        xh, xl = split(x)
+        p.append(dot(xh, high) + dot(xl, high) + dot(xh, low))
+    return p[0][:, :GRID] - p[1][:, GRID:], p[0][:, GRID:] + p[1][:, :GRID]
 
 
 def times_left(ah, al, xr, xi):
     m = ah.shape[0] // 2
-    rh, rl = split(xr)
-    ih, il = split(xi)
-    qr = dot(ah, rh) + dot(al, rh) + dot(ah, rl)
-    qi = dot(ah, ih) + dot(al, ih) + dot(ah, il)
-    return qr[:m] - qi[m:], qr[m:] + qi[:m]
+    xh, xl = split(jnp.concatenate([xr, xi], axis=1))
+    q = []
+    for k in range(2):
+        high, low = ah[k * m : (k + 1) * m], al[k * m : (k + 1) * m]
+        q.append(dot(high, xh) + dot(low, xh) + dot(high, xl))
+    return q[0][:, :GRID] - q[1][:, GRID:], q[1][:, :GRID] + q[0][:, GRID:]
 
 
 def iota_rows(first, count):
@@ -129,8 +132,8 @@
     return lax.axis_index("beam"), t, t % 4, t // 4
 
 
-def prep_body(field, phases, energy, row, col, weight, send, own):
-    _, _, c, _ = place()
+def prep_body(field, phases, energy, row, col, weight, charge, send, own, charges):
+    b, _, c, _ = place()
     for part in range(2):
         for k in range(2):
             send[part * 2 + k] = field[part, 2 + k]
@@ -152,16 +155,11 @@
                     send[4 + 2 * slot + k, at : at + 1, :] = line[:, begin : begin + 256]
     for slot, ref in enumerate((row, col, weight)):
         pick(ref, own_two, 5 + slot)
-
-
-def line_body(charge, charges):
-    b, _, _, _ = place()
-    lane = lax.broadcasted_iota(jnp.int32, (8, 128), 1)
-    line = jnp.zeros((8, 128), f32)
+    lane = lax.broadcasted_iota(jnp.int32, (1, SLICES), 1)
+    line = jnp.zeros((1, SLICES), f32)
     for k in range(4):
         line = jnp.where(lane == 4 * b + k, charge[k].astype(f32) / charge_unit, line)
-    for k in range(BEAM):
-        charges[k] = line
+    charges[...] = line
 
 
 def pack_body(field, received, out):
@@ -194,10 +192,7 @@
     return jnp.where(c < 1, piece, own[slot + 3])
 
 
-def wake_body(gathered, rate, freq, amp, extra):
-    b, _, c, _ = place()
-    g = 4 * b + c
-    charges = jnp.sum(gathered[...], axis=0)
+def wake_sums(g, charges, rate, freq, amp, extra):
     source = lax.broadcasted_iota(jnp.int32, (8, 128), 1)
     pole = lax.broadcasted_iota(jnp.int32, (8, 128), 0)
     rates, freqs, amps = (jnp.zeros((8, 128), f32) for _ in range(3))
@@ -220,8 +215,9 @@
         extra[2 + k] = jnp.broadcast_to(norm, (8, 128))
 
 
-def first_body(x, own, received, extra, states, re, im):
-    _, _, c, _ = place()
+def first_body(x, own, received, charges, rate, freq, amp, states, extra, re, im):
+    b, _, c, _ = place()
+    wake_sums(4 * b + c, charges[...], rate, freq, amp, extra)
     take = functools.partial(period_one, own, received, c)
     fr, fi = whole_field(x, 0), whole_field(x, 1)
     probe(fr, fi, take(2), take(3), re, im)
@@ -235,15 +231,15 @@
     states[1] = energies
 
 
-def second_body(x, states, own, received, extra, high, low, field, re, im):
+def second_body(x, states, own, received, extra, wide, tall, field, re, im):
     b, _, c, _ = place()
     take = functools.partial(period_one, own, received, c)
     br, bi = deposit(states[0], take(4), take(2), take(3))
     strength = deposit_gain * extra[2, 0:1, 0:1]
     fr = deposited(whole_field(x, 0), br, strength)
     fi = deposited(whole_field(x, 1), bi, strength)
-    fr, fi = times_right(fr, fi, high, low)
-    fr, fi = times_left(high[...].reshape(2 * GRID, GRID), low[...].reshape(2 * GRID, GRID), fr, fi)
+    fr, fi = times_right(fr, fi, wide[0], wide[1])
+    fr, fi = times_left(tall[0], tall[1], fr, fi)
     first = (b == 0) & (c == 1)
     fr = jnp.where(first, 0.0, fr)
     fi = jnp.where(first, 0.0, fi)
@@ -264,7 +260,7 @@
     out[1] = energies
 
 
-def fourth_body(field, states, own, received, extra, high, low, out):
+def fourth_body(field, states, own, received, extra, wide, tall, out):
     b, _, c, r = place()
     take = functools.partial(period_two, own, received, c)
     br, bi = deposit(states[0], take(4), take(2), take(3))
@@ -272,10 +268,12 @@
     fr = deposited(field[0], br, strength)
     fi = deposited(field[1], bi, strength)
     at = pl.multiple_of(r * 64, 64)
-    ah = jnp.concatenate([high[0, pl.ds(at, 64), :], high[1, pl.ds(at, 64), :]], axis=0)
-    al = jnp.concatenate([low[0, pl.ds(at, 64), :], low[1, pl.ds(at, 64), :]], axis=0)
+    ah, al = (
+        jnp.concatenate([tall[k, pl.ds(at, 64), :], tall[k, pl.ds(GRID + at, 64), :]], axis=0)
+        for k in range(2)
+    )
     fr, fi = times_left(ah, al, fr, fi)
-    fr, fi = times_right(fr, fi, high, low)
+    fr, fi = times_right(fr, fi, wide[0], wide[1])
     empty = (b == 0) & (c == 0)
     for part, value in enumerate((fr, fi)):
         value = jnp.where(empty, 0.0, value)
@@ -315,38 +313,38 @@
 def shards(
     field_in, phases, energy, row_cell, col_cell, weight, charge, pole_rate, pole_freq, pole_amp
 ):
-    high, low = propagation_table()
-    high, low = jnp.asarray(high), jnp.asarray(low)
+    wide, tall = (jnp.asarray(table) for table in propagation_table())
     kept = (8, ROWS, WIDE)
     state_shape = (2, ROWS, WIDE)
     line = (ROWS, WIDE)
-    send, own = call(
+    send, own, charges = call(
         prep_body,
-        [(14, 16, GRID), kept],
-        field_in, phases, energy, row_cell, col_cell, weight,
-        plain=range(6),
+        [(14, 16, GRID), kept, (1, SLICES)],
+        field_in, phases, energy, row_cell, col_cell, weight, charge,
+        scalars=(6,), plain=range(6),
     )
     received = lax.ppermute(send, "beam", NEXT_BEAM)
-    (charges,) = call(line_body, [(BEAM, 8, 128)], charge, scalars=(0,))
+    charges = jnp.broadcast_to(charges[None], (BEAM, 1, SLICES))
     charges = lax.all_to_all(charges, "beam", 0, 0, tiled=True)
-    (extra,) = call(
-        wake_body, [(4, 8, 128)], charges, pole_rate, pole_freq, pole_amp, scalars=(1, 2, 3)
-    )
+    charges = jnp.sum(charges, axis=0)
     (packed,) = call(pack_body, [(TRANS, 64, 128)], field_in, received, plain=(0,))
     x = lax.all_to_all(packed, "trans", 0, 0, tiled=True)
-    states, _, _ = call(
-        first_body, [state_shape, line, line], x, own, received, extra
+    states, extra, _, _ = call(
+        first_body,
+        [state_shape, (4, 8, 128), line, line],
+        x, own, received, charges, pole_rate, pole_freq, pole_amp,
+        scalars=(4, 5, 6),
     )
     following = lax.ppermute(states, JOINT, TO_PREVIOUS)
     field, re, im = call(
         second_body,
         [(2, GRID, GRID), line, line],
-        x, states, own, received, extra, high, low, plain=(5, 6),
+        x, states, own, received, extra, wide, tall, plain=(5, 6),
     )
     (final,) = call(third_body, [state_shape], following, extra, re, im)
     home = lax.ppermute(final, JOINT, TO_PREVIOUS)
     (bands,) = call(
-        fourth_body, [(4, 32, GRID)], field, final, own, received, extra, high, low, plain=(5, 6)
+        fourth_body, [(4, 32, GRID)], field, final, own, received, extra, wide, tall, plain=(5, 6)
     )
     home = jnp.concatenate([home[..., :256], home[..., 256:]], axis=1).reshape(32, 256)
     both = jnp.concatenate([bands, jnp.broadcast_to(home[None], (4, 32, 256))], axis=1)

time: 82.4 us -> 80.8 us (0.981)
  Pallas kernels: 18 us -> 16.2 us
  waiting for transfers between devices: 25.7 us -> 24 us
    ppermute x1, waiting for transfers between devices: 9.2 us -> 0.01 us  [shards(): received = lax.ppermute(send, 'beam', NEXT_BEAM)]
    all_to_all x1, waiting for transfers between devices: 0.01 us -> 6.78 us  [shards(): charges = lax.all_to_all(charges, 'beam', 0, 0, tiled=True)]
    pallas_call x9 -> x7, Pallas kernels: 18 us -> 16.2 us  [call(): pl.pallas_call(body, out_shape=[kind(shape, f32) for shape in outs], in_s...]
    all_to_all x1, starting transfers between devices: 10.5 us -> 9.38 us  [shards(): charges = lax.all_to_all(charges, 'beam', 0, 0, tiled=True)]
    all_to_all x1, starting transfers between devices: 11.7 us -> 12.7 us  [shards(): x = lax.all_to_all(packed, 'trans', 0, 0, tiled=True)]
  transfers between devices with their start and end apart: 5 -> 5, of which waited for: 3 -> 2; matrix products, arithmetic and copies ran while one was open for 0% -> 1% of each run, Pallas kernels for 16% -> 14%
where the time goes in v5:
time: 80.8 us; the launch traced here: 80.3 us
  starting transfers between devices  29.9 us (37%)
  waiting for transfers between devices  24 us (30%)
  Pallas kernels  16.2 us (20%)
  blocking collectives  8.88 us (11%)
    all_to_all x1, waiting for transfers between devices, shards(): x = lax.all_to_all(packed, 'trans', 0, 0, tiled=True)  17.2 us
    pallas_call x7, Pallas kernels, call(): pl.pallas_call(body, out_shape=[kind(shape, f32) for shape in outs], in_s...  16.2 us
    all_to_all x1, starting transfers between devices, shards(): x = lax.all_to_all(packed, 'trans', 0, 0, tiled=True)  12.7 us
    all_to_all x1, starting transfers between devices, shards(): charges = lax.all_to_all(charges, 'beam', 0, 0, tiled=True)  9.38 us
    all_to_all x1, blocking collectives, shards(): y = lax.all_to_all(both, 'trans', 0, 0, tiled=True, axis_index_groups=QUADS)  8.88 us
    all_to_all x1, waiting for transfers between devices, shards(): charges = lax.all_to_all(charges, 'beam', 0, 0, tiled=True)  6.78 us
    ppermute x1, starting transfers between devices, shards(): received = lax.ppermute(send, 'beam', NEXT_BEAM)  3.94 us
    ppermute x1, starting transfers between devices, shards(): home = lax.ppermute(final, JOINT, TO_PREVIOUS)  1.92 us
  transfers between devices with their start and end apart: 5, of which 2 were waited for; matrix products, arithmetic and copies ran while one was open for 1% of the time, Pallas kernels for 14%

profile of v5, /device:TPU:1, one launch (start us, length us, event | category | flops | bytes accessed | tf_op | source)
XLA Modules:
  0.0 80.3 jit_solution(10562037158300383902)
XLA Ops:
  0.6 1.1 %shard_map.139 = (f32[14,16,256]{2,1,0:T(8,128)S(1)}, f32[8,8,512]{2,1,0:T(8,128)S(1)}, f32[1,128]{1,0:T(1,128)S(1)}) custom-call(f32[2,4,16,256]{3,2,1,0:T(8,128)} %field.3, f32[4,4096]{1,0:T(4,128)} %phases.1, f32[4,4096]{1,0:T(4,128)} %energy.1, s32[4,4096]{1,0:T(4,128)} %row.1, s32[4,4096]{1,0:T(4,128)} %col.1, s32[4,4096]{1,0:T(4,128)} %weight.1, s32[4]{0:T(128)} %charge.1), custom_call_target="tpu_custom_call" | custom-call | tf_op jit(solution)/shard_map/pallas_call | solution.py:305
  1.8 3.9 %collective-permute-start = (f32[14,16,256]{2,1,0:T(8,128)S(1)}, f32[14,16,256]{2,1,0:T(8,128)S(1)}, u32[]{:S(2)}, u32[]{:S(2)}) collective-permute-start(f32[14,16,256]{2,1,0:T(8,128)S(1)} %get-tuple-element.11), channel_id=1, source_target_pairs={{0,16},{16,32},{32,48},{48,64},{64,80},{80,96},{96,112},{112,128},... | collective-permute-start | bytes 688136 | tf_op jit(solution)/shard_map/ppermute | solution.py:326
  5.7 0.6 broadcast_in_dim.16
  6.3 9.4 %all-to-all-start.1 = ((f32[32,1,128]{2,1,0:T(1,128)}), f32[32,1,128]{2,1,0:T(1,128)S(1)}, u32[]{:S(2)}, u32[]{:S(2)}) async-start(f32[32,1,128]{2,1,0:T(1,128)} %broadcast_in_dim.16), calls=%async_computation.1 | async-start | bytes 32768 | tf_op jit(solution)/shard_map/all_to_all | solution.py:328
  15.7 0.0 collective-permute-done.received
  15.7 1.7 %shard_map.140 = f32[16,64,128]{2,1,0:T(8,128)} custom-call(f32[2,4,16,256]{3,2,1,0:T(8,128)} %field.3, f32[14,16,256]{2,1,0:T(8,128)S(1)} %collective-permute-done.received), custom_call_target="tpu_custom_call" | custom-call | tf_op jit(solution)/shard_map/pallas_call | solution.py:305
  17.5 6.8 %all-to-all-done.1 = f32[32,1,128]{2,1,0:T(1,128)S(1)} async-done(((f32[32,1,128]{2,1,0:T(1,128)}), f32[32,1,128]{2,1,0:T(1,128)S(1)}, u32[]{:S(2)}, u32[]{:S(2)}) %all-to-all-start.1) | async-done | bytes 16416 | tf_op jit(solution)/shard_map/all_to_all | solution.py:328
  24.3 12.7 %all-to-all-start = ((f32[16,64,128]{2,1,0:T(8,128)}), f32[16,64,128]{2,1,0:T(8,128)S(1)}, u32[]{:S(2)}, u32[]{:S(2)}) async-start(f32[16,64,128]{2,1,0:T(8,128)} %shard_map.140), calls=%async_computation | async-start | bytes 1048576 | tf_op jit(solution)/shard_map/all_to_all | solution.py:331
  37.0 17.2 %all-to-all-done.x = f32[16,64,128]{2,1,0:T(8,128)S(1)} async-done(((f32[16,64,128]{2,1,0:T(8,128)}), f32[16,64,128]{2,1,0:T(8,128)S(1)}, u32[]{:S(2)}, u32[]{:S(2)}) %all-to-all-start) | async-done | bytes 524320 | tf_op jit(solution)/shard_map/all_to_all | solution.py:331
  54.2 3.4 %shard_map.141 = (f32[2,8,512]{2,1,0:T(8,128)S(1)}, f32[4,8,128]{2,1,0:T(8,128)S(1)}, f32[8,512]{1,0:T(8,128)}, f32[8,512]{1,0:T(8,128)}) custom-call(f32[16,64,128]{2,1,0:T(8,128)S(1)} %all-to-all-done.x, f32[8,8,512]{2,1,0:T(8,128)S(1)} %get-tuple-element.12.own, f32[14,16,256]{2,1,0:T(8,128)S(1)} %collective-permute-done.received, f32[1,128]{1,0:T(1,128)S(1)} %bitcast.4, ...), custom_call_target="tpu_custom_call" | custom-call | tf_op jit(solution)/shard_map/pallas_call | solution.py:305
  57.5 1.9 %collective-permute-start.1 = (f32[2,8,512]{2,1,0:T(8,128)S(1)}, f32[2,8,512]{2,1,0:T(8,128)S(1)}, u32[]{:S(2)}, u32[]{:S(2)}) collective-permute-start(f32[2,8,512]{2,1,0:T(8,128)S(1)} %get-tuple-element.14.states), channel_id=1, source_target_pairs={{0,499},{1,0},{2,1},{3,2},{4,503},{5,4},{6,5},{7,6},{8,507},{9,8},... | collective-permute-start | bytes 98312 | tf_op jit(solution)/shard_map/ppermute | solution.py:338
  59.5 5.7 %shard_map.142 = (f32[2,256,256]{2,1,0:T(8,128)S(1)}, f32[8,512]{1,0:T(8,128)S(1)}, f32[8,512]{1,0:T(8,128)S(1)}) custom-call(f32[16,64,128]{2,1,0:T(8,128)S(1)} %all-to-all-done.x, f32[2,8,512]{2,1,0:T(8,128)S(1)} %get-tuple-element.14.states, f32[8,8,512]{2,1,0:T(8,128)S(1)} %get-tuple-element.12.own, f32[14,16,256]{2,1,0:T(8,128)S(1)} %collective-permute-done.received, ...), custom_call_target="tpu_custom_call" | custom-call | tf_op jit(solution)/shard_map/pallas_call | solution.py:305
  65.2 0.0 collective-permute-done.1.states
  65.2 0.1 shard_map.143.states
  65.3 1.9 %collective-permute-start.2 = (f32[2,8,512]{2,1,0:T(8,128)S(1)}, f32[2,8,512]{2,1,0:T(8,128)S(1)}, u32[]{:S(2)}, u32[]{:S(2)}) collective-permute-start(f32[2,8,512]{2,1,0:T(8,128)S(1)} %shard_map.143.states), channel_id=1, source_target_pairs={{0,499},{1,0},{2,1},{3,2},{4,503},{5,4},{6,5},{7,6},{8,507},{9,8},... | collective-permute-start | bytes 98312 | tf_op jit(solution)/shard_map/ppermute | solution.py:345
  67.2 3.4 %shard_map.144 = f32[4,32,256]{2,1,0:T(8,128)S(1)} custom-call(f32[2,256,256]{2,1,0:T(8,128)S(1)} %get-tuple-element.16.field, f32[2,8,512]{2,1,0:T(8,128)S(1)} %shard_map.143.states, f32[8,8,512]{2,1,0:T(8,128)S(1)} %get-tuple-element.12.own, f32[14,16,256]{2,1,0:T(8,128)S(1)} %collective-permute-done.received, f32[4,8,128]{2,1,0:T(8,128)S(1)} %get-tuple-element.15.extra, ...), custom_call_target="tpu_custom_call" | custom-call | tf_op jit(solution)/shard_map/pallas_call | solution.py:305
  70.6 0.0 collective-permute-done.2
  70.7 8.9 %all_to_all.15.x = f32[4,64,256]{2,1,0:T(8,128)S(1)} all-to-all(f32[4,64,256]{2,1,0:T(8,128)S(1)} %pad_maximum_fusion), channel_id=1, replica_groups={{0,1,2,3},{4,5,6,7},{8,9,10,11},{12,13,14,15},{16,17,18,19},{20,21,22,2..., dimensions={0} | all-to-all | bytes 524288 | tf_op jit(solution)/shard_map/all_to_all | solution.py:351
  79.6 0.7 shard_map.145
  (5 shorter events, 0.1 us)
Async XLA Ops:
  1.8 13.9 %collective-permute-start = (f32[14,16,256]{2,1,0:T(8,128)S(1)}, f32[14,16,256]{2,1,0:T(8,128)S(1)}, u32[]{:S(2)}, u32[]{:S(2)}) collective-permute-start(f32[14,16,256]{2,1,0:T(8,128)S(1)} %get-tuple-element.11), channel_id=1, source_target_pairs={{0,16},{16,32},{32,48},{48,64},{64,80},{80,96},{96,112},{112,128},... | collective-permute-start | bytes 688136 | tf_op jit(solution)/shard_map/ppermute | solution.py:326
  6.3 17.9 %all-to-all-start.1 = ((f32[32,1,128]{2,1,0:T(1,128)}), f32[32,1,128]{2,1,0:T(1,128)S(1)}, u32[]{:S(2)}, u32[]{:S(2)}) async-start(f32[32,1,128]{2,1,0:T(1,128)} %broadcast_in_dim.16), calls=%async_computation.1 | async-start | bytes 32768 | tf_op jit(solution)/shard_map/all_to_all | solution.py:328
  24.3 29.9 %all-to-all-start = ((f32[16,64,128]{2,1,0:T(8,128)}), f32[16,64,128]{2,1,0:T(8,128)S(1)}, u32[]{:S(2)}, u32[]{:S(2)}) async-start(f32[16,64,128]{2,1,0:T(8,128)} %shard_map.140), calls=%async_computation | async-start | bytes 1048576 | tf_op jit(solution)/shard_map/all_to_all | solution.py:331
  57.5 7.6 %collective-permute-start.1 = (f32[2,8,512]{2,1,0:T(8,128)S(1)}, f32[2,8,512]{2,1,0:T(8,128)S(1)}, u32[]{:S(2)}, u32[]{:S(2)}) collective-permute-start(f32[2,8,512]{2,1,0:T(8,128)S(1)} %get-tuple-element.14.states), channel_id=1, source_target_pairs={{0,499},{1,0},{2,1},{3,2},{4,503},{5,4},{6,5},{7,6},{8,507},{9,8},... | collective-permute-start | bytes 98312 | tf_op jit(solution)/shard_map/ppermute | solution.py:338
  65.3 5.4 %collective-permute-start.2 = (f32[2,8,512]{2,1,0:T(8,128)S(1)}, f32[2,8,512]{2,1,0:T(8,128)S(1)}, u32[]{:S(2)}, u32[]{:S(2)}) collective-permute-start(f32[2,8,512]{2,1,0:T(8,128)S(1)} %shard_map.143.states), channel_id=1, source_target_pairs={{0,499},{1,0},{2,1},{3,2},{4,503},{5,4},{6,5},{7,6},{8,507},{9,8},... | collective-permute-start | bytes 98312 | tf_op jit(solution)/shard_map/ppermute | solution.py:345

commit v6 on v5

--- a/solution.py
+++ b/solution.py
@@ -21,6 +21,7 @@
 TRANS = 16
 LOW, HIGH = 32, 224
 SPAN = HIGH - LOW
+TABLE = (2, 2 * GRID, GRID)
 ROWS, WIDE = 8, 512
 JOINT = ("beam", "trans")
 QUADS = [[4 * r + c for c in range(4)] for r in range(4)]
@@ -38,9 +39,7 @@
     parts = np.stack([a.real, a.imag]).astype(np.float32)
     high = parts.astype(jnp.bfloat16)
     low = (parts - high.astype(np.float32)).astype(jnp.bfloat16)
-    tall = np.stack([part.reshape(2 * GRID, GRID) for part in (high, low)])
-    wide = np.stack([np.concatenate([part[0], part[1]], axis=1) for part in (high, low)])
-    return wide, tall
+    return np.stack([part.reshape(2 * GRID, GRID) for part in (high, low)])
 
 
 def moved(fn):
@@ -69,8 +68,10 @@
     p = []
     for x in (xr, xi):
         xh, xl = split(x)
-        p.append(dot(xh, high) + dot(xl, high) + dot(xh, low))
-    return p[0][:, :GRID] - p[1][:, GRID:], p[0][:, GRID:] + p[1][:, :GRID]
+        for k in range(2):
+            h, w = high[k * GRID : (k + 1) * GRID], low[k * GRID : (k + 1) * GRID]
+            p.append(dot(xh, h) + dot(xl, h) + dot(xh, w))
+    return p[0] - p[3], p[1] + p[2]
 
 
 def times_left(ah, al, xr, xi):
@@ -231,14 +232,15 @@
     states[1] = energies
 
 
-def second_body(x, states, own, received, extra, wide, tall, field, re, im):
+def second_body(x, states, own, received, extra, tall, field, re, im, again):
+    again[...] = tall[...]
     b, _, c, _ = place()
     take = functools.partial(period_one, own, received, c)
     br, bi = deposit(states[0], take(4), take(2), take(3))
     strength = deposit_gain * extra[2, 0:1, 0:1]
     fr = deposited(whole_field(x, 0), br, strength)
     fi = deposited(whole_field(x, 1), bi, strength)
-    fr, fi = times_right(fr, fi, wide[0], wide[1])
+    fr, fi = times_right(fr, fi, tall[0], tall[1])
     fr, fi = times_left(tall[0], tall[1], fr, fi)
     first = (b == 0) & (c == 1)
     fr = jnp.where(first, 0.0, fr)
@@ -260,7 +262,7 @@
     out[1] = energies
 
 
-def fourth_body(field, states, own, received, extra, wide, tall, out):
+def fourth_body(field, states, own, received, extra, tall, out):
     b, _, c, r = place()
     take = functools.partial(period_two, own, received, c)
     br, bi = deposit(states[0], take(4), take(2), take(3))
@@ -273,7 +275,7 @@
         for k in range(2)
     )
     fr, fi = times_left(ah, al, fr, fi)
-    fr, fi = times_right(fr, fi, wide[0], wide[1])
+    fr, fi = times_right(fr, fi, tall[0], tall[1])
     empty = (b == 0) & (c == 0)
     for part, value in enumerate((fr, fi)):
         value = jnp.where(empty, 0.0, value)
@@ -294,7 +296,7 @@
                     target[c : c + 1, begin : begin + 256] = piece[q : q + 1]
 
 
-def call(body, outs, *args, scalars=(), plain=(), last=False):
+def call(body, outs, *args, scalars=(), plain=(), last=False, room=0):
     specs, inputs = [], []
     for k, arg in enumerate(args):
         specs.append(pl.BlockSpec(memory_space=pltpu.SMEM if k in scalars else pltpu.VMEM))
@@ -304,16 +306,17 @@
     kind = jax.ShapeDtypeStruct if last else pltpu.VMEM
     return pl.pallas_call(
         body,
-        out_shape=[kind(shape, f32) for shape in outs],
+        out_shape=[kind(shape, bf16 if shape == TABLE else f32) for shape in outs],
         in_specs=specs,
         out_specs=[pl.BlockSpec(memory_space=pltpu.VMEM) for _ in outs],
+        compiler_params=pltpu.CompilerParams(vmem_limit_bytes=room << 20) if room else None,
     )(*inputs)
 
 
 def shards(
     field_in, phases, energy, row_cell, col_cell, weight, charge, pole_rate, pole_freq, pole_amp
 ):
-    wide, tall = (jnp.asarray(table) for table in propagation_table())
+    tall = jnp.asarray(propagation_table())
     kept = (8, ROWS, WIDE)
     state_shape = (2, ROWS, WIDE)
     line = (ROWS, WIDE)
@@ -327,7 +330,7 @@
     charges = jnp.broadcast_to(charges[None], (BEAM, 1, SLICES))
     charges = lax.all_to_all(charges, "beam", 0, 0, tiled=True)
     charges = jnp.sum(charges, axis=0)
-    (packed,) = call(pack_body, [(TRANS, 64, 128)], field_in, received, plain=(0,))
+    (packed,) = call(pack_body, [(TRANS, 64, 128)], field_in, received)
     x = lax.all_to_all(packed, "trans", 0, 0, tiled=True)
     states, extra, _, _ = call(
         first_body,
@@ -336,15 +339,15 @@
         scalars=(4, 5, 6),
     )
     following = lax.ppermute(states, JOINT, TO_PREVIOUS)
-    field, re, im = call(
+    field, re, im, tall = call(
         second_body,
-        [(2, GRID, GRID), line, line],
-        x, states, own, received, extra, wide, tall, plain=(5, 6),
-    )
-    (final,) = call(third_body, [state_shape], following, extra, re, im)
+        [(2, GRID, GRID), line, line, TABLE],
+        x, states, own, received, extra, tall, room=24,
+    )
+    (final,) = call(third_body, [state_shape], following, extra, re, im, room=24)
     home = lax.ppermute(final, JOINT, TO_PREVIOUS)
     (bands,) = call(
-        fourth_body, [(4, 32, GRID)], field, final, own, received, extra, wide, tall, plain=(5, 6)
+        fourth_body, [(4, 32, GRID)], field, final, own, received, extra, tall, room=24
     )
     home = jnp.concatenate([home[..., :256], home[..., 256:]], axis=1).reshape(32, 256)
     both = jnp.concatenate([bands, jnp.broadcast_to(home[None], (4, 32, 256))], axis=1)

time: 80.8 us -> 79.5 us (0.984)
  Pallas kernels: 16.2 us -> 12.9 us
  waiting for transfers between devices: 24 us -> 25.9 us
    pallas_call x7, Pallas kernels: 16.2 us -> 12.9 us  [call(): pl.pallas_call(body, out_shape=[kind(shape, bf16 if shape == TABLE else f...]
    ppermute x1, waiting for transfers between devices: 0.01 us -> 1.05 us  [shards(): home = lax.ppermute(final, JOINT, TO_PREVIOUS)]
    all_to_all x1, waiting for transfers between devices: 6.78 us -> 7.69 us  [shards(): charges = lax.all_to_all(charges, 'beam', 0, 0, tiled=True)]
  transfers between devices with their start and end apart: 5 -> 5, of which waited for: 2 -> 3; matrix products, arithmetic and copies ran while one was open for 1% -> 1% of each run, Pallas kernels for 14% -> 10%
where the time goes in v6:
time: 79.5 us; the launch traced here: 79.2 us
  starting transfers between devices  29.9 us (38%)
  waiting for transfers between devices  25.9 us (33%)
  Pallas kernels  12.9 us (16%)
  blocking collectives  9.04 us (11%)
    all_to_all x1, waiting for transfers between devices, shards(): x = lax.all_to_all(packed, 'trans', 0, 0, tiled=True)  17.2 us
    pallas_call x7, Pallas kernels, call(): pl.pallas_call(body, out_shape=[kind(shape, bf16 if shape == TABLE else f...  12.9 us
    all_to_all x1, starting transfers between devices, shards(): x = lax.all_to_all(packed, 'trans', 0, 0, tiled=True)  12.7 us
    all_to_all x1, starting transfers between devices, shards(): charges = lax.all_to_all(charges, 'beam', 0, 0, tiled=True)  9.38 us
    all_to_all x1, blocking collectives, shards(): y = lax.all_to_all(both, 'trans', 0, 0, tiled=True, axis_index_groups=QUADS)  9.04 us
    all_to_all x1, waiting for transfers between devices, shards(): charges = lax.all_to_all(charges, 'beam', 0, 0, tiled=True)  7.69 us
    ppermute x1, starting transfers between devices, shards(): received = lax.ppermute(send, 'beam', NEXT_BEAM)  3.94 us
    ppermute x1, starting transfers between devices, shards(): home = lax.ppermute(final, JOINT, TO_PREVIOUS)  1.92 us
  transfers between devices with their start and end apart: 5, of which 3 were waited for; matrix products, arithmetic and copies ran while one was open for 1% of the time, Pallas kernels for 10%

profile of v6, /device:TPU:1, one launch (start us, length us, event | category | flops | bytes accessed | tf_op | source)
XLA Modules:
  0.0 79.2 jit_solution(11952572063743270911)
XLA Ops:
  0.6 0.0 copy-start
  0.6 1.2 %shard_map.130 = (f32[14,16,256]{2,1,0:T(8,128)S(1)}, f32[8,8,512]{2,1,0:T(8,128)S(1)}, f32[1,128]{1,0:T(1,128)S(1)}) custom-call(f32[2,4,16,256]{3,2,1,0:T(8,128)} %field.3, f32[4,4096]{1,0:T(4,128)} %phases.1, f32[4,4096]{1,0:T(4,128)} %energy.1, s32[4,4096]{1,0:T(4,128)} %row.1, s32[4,4096]{1,0:T(4,128)} %col.1, s32[4,4096]{1,0:T(4,128)} %weight.1, s32[4]{0:T(128)} %charge.1), custom_call_target="tpu_custom_call" | custom-call | tf_op jit(solution)/shard_map/pallas_call | solution.py:307
  1.8 3.9 %collective-permute-start = (f32[14,16,256]{2,1,0:T(8,128)S(1)}, f32[14,16,256]{2,1,0:T(8,128)S(1)}, u32[]{:S(2)}, u32[]{:S(2)}) collective-permute-start(f32[14,16,256]{2,1,0:T(8,128)S(1)} %get-tuple-element.12), channel_id=1, source_target_pairs={{0,16},{16,32},{32,48},{48,64},{64,80},{80,96},{96,112},{112,128},... | collective-permute-start | bytes 688136 | tf_op jit(solution)/shard_map/ppermute | solution.py:329
  5.8 0.6 broadcast_in_dim.16
  6.4 9.4 %all-to-all-start.1 = ((f32[32,1,128]{2,1,0:T(1,128)}), f32[32,1,128]{2,1,0:T(1,128)S(1)}, u32[]{:S(2)}, u32[]{:S(2)}) async-start(f32[32,1,128]{2,1,0:T(1,128)} %broadcast_in_dim.16), calls=%async_computation.1 | async-start | bytes 32768 | tf_op jit(solution)/shard_map/all_to_all | solution.py:331
  15.8 0.0 collective-permute-done.received
  15.8 0.0 copy-done
  15.8 0.8 %shard_map.131 = f32[16,64,128]{2,1,0:T(8,128)} custom-call(f32[2,4,16,256]{3,2,1,0:T(8,128)S(1)} %copy-done, f32[14,16,256]{2,1,0:T(8,128)S(1)} %collective-permute-done.received), custom_call_target="tpu_custom_call" | custom-call | tf_op jit(solution)/shard_map/pallas_call | solution.py:307
  16.6 7.7 %all-to-all-done.1 = f32[32,1,128]{2,1,0:T(1,128)S(1)} async-done(((f32[32,1,128]{2,1,0:T(1,128)}), f32[32,1,128]{2,1,0:T(1,128)S(1)}, u32[]{:S(2)}, u32[]{:S(2)}) %all-to-all-start.1) | async-done | bytes 16416 | tf_op jit(solution)/shard_map/all_to_all | solution.py:331
  24.3 12.7 %all-to-all-start = ((f32[16,64,128]{2,1,0:T(8,128)}), f32[16,64,128]{2,1,0:T(8,128)S(1)}, u32[]{:S(2)}, u32[]{:S(2)}) async-start(f32[16,64,128]{2,1,0:T(8,128)} %shard_map.131), calls=%async_computation | async-start | bytes 1048576 | tf_op jit(solution)/shard_map/all_to_all | solution.py:334
  37.0 0.0 copy-start.1
  37.0 17.2 %all-to-all-done.x = f32[16,64,128]{2,1,0:T(8,128)S(1)} async-done(((f32[16,64,128]{2,1,0:T(8,128)}), f32[16,64,128]{2,1,0:T(8,128)S(1)}, u32[]{:S(2)}, u32[]{:S(2)}) %all-to-all-start) | async-done | bytes 524320 | tf_op jit(solution)/shard_map/all_to_all | solution.py:334
  54.2 3.3 %shard_map.132 = (f32[2,8,512]{2,1,0:T(8,128)S(1)}, f32[4,8,128]{2,1,0:T(8,128)S(1)}, f32[8,512]{1,0:T(8,128)}, f32[8,512]{1,0:T(8,128)}) custom-call(f32[16,64,128]{2,1,0:T(8,128)S(1)} %all-to-all-done.x, f32[8,8,512]{2,1,0:T(8,128)S(1)} %get-tuple-element.13.own, f32[14,16,256]{2,1,0:T(8,128)S(1)} %collective-permute-done.received, f32[1,128]{1,0:T(1,128)S(1)} %bitcast.4, ...), custom_call_target="tpu_custom_call" | custom-call | tf_op jit(solution)/shard_map/pallas_call | solution.py:307
  57.6 1.9 %collective-permute-start.1 = (f32[2,8,512]{2,1,0:T(8,128)S(1)}, f32[2,8,512]{2,1,0:T(8,128)S(1)}, u32[]{:S(2)}, u32[]{:S(2)}) collective-permute-start(f32[2,8,512]{2,1,0:T(8,128)S(1)} %get-tuple-element.15.states), channel_id=1, source_target_pairs={{0,499},{1,0},{2,1},{3,2},{4,503},{5,4},{6,5},{7,6},{8,507},{9,8},... | collective-permute-start | bytes 98312 | tf_op jit(solution)/shard_map/ppermute | solution.py:341
  59.5 0.0 copy-done.1
  59.5 4.5 %shard_map.133 = (f32[2,256,256]{2,1,0:T(8,128)S(1)}, f32[8,512]{1,0:T(8,128)S(1)}, f32[8,512]{1,0:T(8,128)S(1)}, bf16[2,512,256]{2,1,0:T(8,128)(2,1)S(1)}) custom-call(f32[16,64,128]{2,1,0:T(8,128)S(1)} %all-to-all-done.x, f32[2,8,512]{2,1,0:T(8,128)S(1)} %get-tuple-element.15.states, f32[8,8,512]{2,1,0:T(8,128)S(1)} %get-tuple-element.13.own, ...), custom_call_target="tpu_custom_call" | custom-call | tf_op jit(solution)/shard_map/pallas_call | solution.py:307
  64.0 0.0 collective-permute-done.1.states
  64.0 0.1 shard_map.134.states
  64.1 1.9 %collective-permute-start.2 = (f32[2,8,512]{2,1,0:T(8,128)S(1)}, f32[2,8,512]{2,1,0:T(8,128)S(1)}, u32[]{:S(2)}, u32[]{:S(2)}) collective-permute-start(f32[2,8,512]{2,1,0:T(8,128)S(1)} %shard_map.134.states), channel_id=1, source_target_pairs={{0,499},{1,0},{2,1},{3,2},{4,503},{5,4},{6,5},{7,6},{8,507},{9,8},... | collective-permute-start | bytes 98312 | tf_op jit(solution)/shard_map/ppermute | solution.py:348
  66.0 2.2 %shard_map.135 = f32[4,32,256]{2,1,0:T(8,128)S(1)} custom-call(f32[2,256,256]{2,1,0:T(8,128)S(1)} %get-tuple-element.17.field, f32[2,8,512]{2,1,0:T(8,128)S(1)} %shard_map.134.states, f32[8,8,512]{2,1,0:T(8,128)S(1)} %get-tuple-element.13.own, f32[14,16,256]{2,1,0:T(8,128)S(1)} %collective-permute-done.received, f32[4,8,128]{2,1,0:T(8,128)S(1)} %get-tuple-element.16.extra, ...), custom_call_target="tpu_custom_call" | custom-call | tf_op jit(solution)/shard_map/pallas_call | solution.py:307
  68.3 1.1 %collective-permute-done.2 = f32[2,8,512]{2,1,0:T(8,128)S(1)} collective-permute-done((f32[2,8,512]{2,1,0:T(8,128)S(1)}, f32[2,8,512]{2,1,0:T(8,128)S(1)}, u32[]{:S(2)}, u32[]{:S(2)}) %collective-permute-start.2) | collective-permute-done | bytes 32800 | tf_op jit(solution)/shard_map/ppermute | solution.py:348
  69.4 9.0 %all_to_all.15.x = f32[4,64,256]{2,1,0:T(8,128)S(1)} all-to-all(f32[4,64,256]{2,1,0:T(8,128)S(1)} %pad_maximum_fusion), channel_id=1, replica_groups={{0,1,2,3},{4,5,6,7},{8,9,10,11},{12,13,14,15},{16,17,18,19},{20,21,22,2..., dimensions={0} | all-to-all | bytes 524288 | tf_op jit(solution)/shard_map/all_to_all | solution.py:354
  78.4 0.7 shard_map.136
  (5 shorter events, 0.1 us)
Async XLA Ops:
  0.6 15.1 %copy-start = (f32[2,4,16,256]{3,2,1,0:T(8,128)S(1)}, f32[2,4,16,256]{3,2,1,0:T(8,128)}, u32[]{:S(2)}) copy-start(f32[2,4,16,256]{3,2,1,0:T(8,128)} %field.3) | copy-start | bytes 393220
  1.8 13.9 %collective-permute-start = (f32[14,16,256]{2,1,0:T(8,128)S(1)}, f32[14,16,256]{2,1,0:T(8,128)S(1)}, u32[]{:S(2)}, u32[]{:S(2)}) collective-permute-start(f32[14,16,256]{2,1,0:T(8,128)S(1)} %get-tuple-element.12), channel_id=1, source_target_pairs={{0,16},{16,32},{32,48},{48,64},{64,80},{80,96},{96,112},{112,128},... | collective-permute-start | bytes 688136 | tf_op jit(solution)/shard_map/ppermute | solution.py:329
  6.4 17.9 %all-to-all-start.1 = ((f32[32,1,128]{2,1,0:T(1,128)}), f32[32,1,128]{2,1,0:T(1,128)S(1)}, u32[]{:S(2)}, u32[]{:S(2)}) async-start(f32[32,1,128]{2,1,0:T(1,128)} %broadcast_in_dim.16), calls=%async_computation.1 | async-start | bytes 32768 | tf_op jit(solution)/shard_map/all_to_all | solution.py:331
  24.3 29.9 %all-to-all-start = ((f32[16,64,128]{2,1,0:T(8,128)}), f32[16,64,128]{2,1,0:T(8,128)S(1)}, u32[]{:S(2)}, u32[]{:S(2)}) async-start(f32[16,64,128]{2,1,0:T(8,128)} %shard_map.131), calls=%async_computation | async-start | bytes 1048576 | tf_op jit(solution)/shard_map/all_to_all | solution.py:334
  37.0 22.5 %copy-start.1 = (bf16[2,512,256]{2,1,0:T(8,128)(2,1)S(1)}, bf16[2,512,256]{2,1,0:T(8,128)(2,1)}, u32[]{:S(2)}) copy-start(bf16[2,512,256]{2,1,0:T(8,128)(2,1)} %constant.4.clone.tall) | copy-start | bytes 1572868
  57.6 6.5 %collective-permute-start.1 = (f32[2,8,512]{2,1,0:T(8,128)S(1)}, f32[2,8,512]{2,1,0:T(8,128)S(1)}, u32[]{:S(2)}, u32[]{:S(2)}) collective-permute-start(f32[2,8,512]{2,1,0:T(8,128)S(1)} %get-tuple-element.15.states), channel_id=1, source_target_pairs={{0,499},{1,0},{2,1},{3,2},{4,503},{5,4},{6,5},{7,6},{8,507},{9,8},... | collective-permute-start | bytes 98312 | tf_op jit(solution)/shard_map/ppermute | solution.py:341
  64.1 5.2 %collective-permute-start.2 = (f32[2,8,512]{2,1,0:T(8,128)S(1)}, f32[2,8,512]{2,1,0:T(8,128)S(1)}, u32[]{:S(2)}, u32[]{:S(2)}) collective-permute-start(f32[2,8,512]{2,1,0:T(8,128)S(1)} %shard_map.134.states), channel_id=1, source_target_pairs={{0,499},{1,0},{2,1},{3,2},{4,503},{5,4},{6,5},{7,6},{8,507},{9,8},... | collective-permute-start | bytes 98312 | tf_op jit(solution)/shard_map/ppermute | solution.py:348
